TPU v7x, 512 devices: a whole 4x8x8 slice. The times are simulated.
512 devices in a mesh: shot: 32 (over z, x_lo, core), dom: 16 (over y, x_hi).
Axes of the slice: x: 4 (x_hi: 2, x_lo: 2; x = x_hi * 2 + x_lo), y: 8, z: 8, core: 2. Of those that a mesh axis runs over, the one named last changes fastest.
Arguments:
- kappa: float32 [32, 512, 128], P('dom'), may hold values from 0.05 to 0.15
- wave_now: float32 [32, 32, 512, 128], P('shot', 'dom'), may hold values from -6 to 6
- wave_before: float32 [32, 32, 512, 128], P('shot', 'dom'), may hold values from -6 to 6
- wavelet: float32 [32, 4], P('shot'), may hold values from -8 to 8
- source_cell: int32 [32], P('shot'), may hold values from 0 to 2097151
- receiver_cells: int32 [32, 2048], P('shot'), may hold values from 0 to 2097151
- observed: float32 [32, 4, 2048], P('shot'), may hold values from -6 to 6
Outputs:
- total_gradient: float32 [32, 512, 128], P('dom', 'shot')
- wave_next: float32 [32, 32, 512, 128], P('shot', 'dom')
Inputs may be any that keep to these rules, and one draw needn't show every extreme that they name: `source_cell`: a cell index x * 512 * 128 + y * 128 + z. `receiver_cells`: cell indices x * 512 * 128 + y * 128 + z; a cell may hold several receivers.
All inputs are finite; a program needn't handle non-finite values.
Results may differ from a plain program's by a relative error of at most 0.00013.
Values sent between devices are 32-bit elements; how exact they have to be, the bound alone decides.
A program may use at most 64 MiB of HBM per device.

v0:
```python
import jax
import jax.numpy as jnp
from jax import lax
from jax.sharding import PartitionSpec as P

NT = 4


PRIOR_GAIN = 50.0


def with_halo(cells, sides, width):
    for axis, dim in sides:
        count = lax.axis_size(axis)
        ends = count - 1
        head = lax.slice_in_dim(cells, 0, width, axis=dim)
        tail = lax.slice_in_dim(cells, cells.shape[dim] - width, cells.shape[dim], axis=dim)
        cells = jnp.concatenate(
            [
                lax.ppermute(tail, axis, [(i, (i + 1) % count) for i in range(ends)]),
                cells,
                lax.ppermute(head, axis, [((i + 1) % count, i) for i in range(ends)]),
            ],
            axis=dim,
        )
    return cells


def neighbours(padded):
    core = padded[..., 1:-1, :, :]
    widths = [(0, 0)] * (core.ndim - 2) + [(1, 1), (1, 1)]
    flank = jnp.pad(core, widths)
    total = padded[..., 2:, :, :] + padded[..., :-2, :, :]
    total = total + flank[..., 2:, 1:-1] + flank[..., :-2, 1:-1]
    total = total + flank[..., 1:-1, 2:] + flank[..., 1:-1, :-2]
    return total


def shards(kappa, wave_now, wave_before, wavelet, source_cell, receiver_cells, observed):
    shots, planes, rows_y, depth = wave_now.shape
    cells = planes * rows_y * depth
    offset = lax.axis_index("dom") * cells
    source_local = source_cell - offset
    source_mine = (source_local >= 0) & (source_local < cells)
    source_at = jnp.clip(source_local, 0, cells - 1)
    receiver_local = receiver_cells - offset
    receiver_mine = (receiver_local >= 0) & (receiver_local < cells)
    receiver_at = jnp.clip(receiver_local, 0, cells - 1)
    shot_rows = jnp.arange(shots)

    def inject_misfit(field, miss):
        flat = field.reshape(shots, cells)
        flat = flat.at[shot_rows[:, None], receiver_at].add(miss)
        return flat.reshape(field.shape)

    now, before = (wave_now, wave_before)
    history = []
    residues = []
    lap = now
    for step in range(NT):
        forward_padded = with_halo(now, (("dom", 1),), 1)
        lap = neighbours(forward_padded) - 6.0 * now
        history.append(lap)
        after = 2.0 * now - before + kappa * lap
        inject_flat = after.reshape(shots, cells)
        inject_flat = inject_flat.at[shot_rows, source_at].add(
            jnp.where(source_mine, wavelet[:, step], 0.0)
        )
        after = inject_flat.reshape(after.shape)
        misfit_flat = after.reshape(shots, cells)
        taken = jnp.take_along_axis(misfit_flat, receiver_at, axis=1)
        residues.append(jnp.where(receiver_mine, taken - observed[:, step], 0.0))
        before, now = (now, after)
    zeros = jnp.zeros_like(now)
    adjoint_next = inject_misfit(zeros, residues[NT - 1])
    adjoint_after = zeros
    image = jnp.sum(adjoint_next * history[NT - 1], axis=0)
    for level in range(NT - 1, 0, -1):
        weighted = kappa * adjoint_next
        padded = with_halo(weighted, (("dom", 1),), 1)
        lap_weighted = neighbours(padded) - 6.0 * weighted
        adjoint_now = 2.0 * adjoint_next + lap_weighted - adjoint_after
        adjoint_now = inject_misfit(adjoint_now, residues[level - 1])
        image = image + jnp.sum(adjoint_now * history[level - 1], axis=0)
        adjoint_after, adjoint_next = (adjoint_next, adjoint_now)
    owned = lax.psum_scatter(image, "shot", scatter_dimension=1, tiled=True)
    band = owned.shape[1]
    start = lax.axis_index("shot") * band
    widened = jnp.pad(kappa, ((0, 0), (1, 1), (0, 0)))
    strip = lax.dynamic_slice_in_dim(widened, start, band + 2, 1)
    rim = with_halo(strip, (("dom", 0),), 1)
    core = rim[1:-1, 1:-1]
    flank = jnp.pad(core, ((0, 0), (0, 0), (1, 1)))
    total = rim[2:, 1:-1] + rim[:-2, 1:-1]
    total = total + rim[1:-1, 2:] + rim[1:-1, :-2]
    total = total + flank[..., 2:] + flank[..., :-2]
    smooth = total / 6.0
    score = (smooth - core) * PRIOR_GAIN
    total_gradient = owned / NT - score
    return (total_gradient, now)


def solution(mesh):
    return jax.shard_map(
        shards,
        mesh=mesh,
        in_specs=(
            P("dom", None, None),
            P("shot", "dom", None, None),
            P("shot", "dom", None, None),
            P("shot", None),
            P("shot"),
            P("shot", None),
            P("shot", None, None),
        ),
        out_specs=(P("dom", "shot", None), P("shot", "dom", None, None)),
        check_vma=False,
    )
```

profile of v0, /device:TPU:1, one launch (start us, length us, event | category | flops | bytes accessed | tf_op | source)
XLA Modules:
  0.0 374.1 jit_solution(8442021232092566591)
XLA Ops:
  9.7 6.1 %collective-permute-start.1 = (f32[1,1,512,128]{3,2,1,0:T(8,128)S(1)}, f32[1,1,512,128]{3,2,1,0:T(8,128)S(1)}, u32[]{:S(2)}, u32[]{:S(2)}) collective-permute-start(f32[1,1,512,128]{3,2,1,0:T(8,128)S(1)} %get-tuple-element.74), channel_id=1, source_target_pairs={{0,1},{1,2},{2,3},{3,4},{4,5},{5,6},{6,7},{7,8},{8,9},{9,10},{10,1... | collective-permute-start | bytes 786440 | tf_op jit(solution)/shard_map/ppermute | solution.py:20
  19.3 4.8 %collective-permute-done.1 = f32[1,1,512,128]{3,2,1,0:T(8,128)S(1)} collective-permute-done((f32[1,1,512,128]{3,2,1,0:T(8,128)S(1)}, f32[1,1,512,128]{3,2,1,0:T(8,128)S(1)}, u32[]{:S(2)}, u32[]{:S(2)}) %collective-permute-start.1) | collective-permute-done | bytes 262176 | tf_op jit(solution)/shard_map/ppermute | solution.py:20
  24.0 1.4 fusion.47
  29.4 6.3 %collective-permute-start.3 = (f32[1,1,512,128]{3,2,1,0:T(8,128)S(1)}, f32[1,1,512,128]{3,2,1,0:T(8,128)S(1)}, u32[]{:S(2)}, u32[]{:S(2)}) collective-permute-start(f32[1,1,512,128]{3,2,1,0:T(8,128)S(1)} %get-tuple-element.72), channel_id=1, source_target_pairs={{0,1},{1,2},{2,3},{3,4},{4,5},{5,6},{6,7},{7,8},{8,9},{9,10},{10,1... | collective-permute-start | bytes 786440 | tf_op jit(solution)/shard_map/ppermute | solution.py:20
  35.7 1.8 collective-permute-done.2
  37.5 8.3 %collective-permute-done.3 = f32[1,1,512,128]{3,2,1,0:T(8,128)S(1)} collective-permute-done((f32[1,1,512,128]{3,2,1,0:T(8,128)S(1)}, f32[1,1,512,128]{3,2,1,0:T(8,128)S(1)}, u32[]{:S(2)}, u32[]{:S(2)}) %collective-permute-start.3) | collective-permute-done | bytes 262176 | tf_op jit(solution)/shard_map/ppermute | solution.py:20
  49.6 1.3 collective-permute-start.4
  50.9 6.3 %collective-permute-start.5 = (f32[1,1,512,128]{3,2,1,0:T(8,128)S(1)}, f32[1,1,512,128]{3,2,1,0:T(8,128)S(1)}, u32[]{:S(2)}, u32[]{:S(2)}) collective-permute-start(f32[1,1,512,128]{3,2,1,0:T(8,128)S(1)} %get-tuple-element.70), channel_id=1, source_target_pairs={{0,1},{1,2},{2,3},{3,4},{4,5},{5,6},{6,7},{7,8},{8,9},{9,10},{10,1... | collective-permute-start | bytes 786440 | tf_op jit(solution)/shard_map/ppermute | solution.py:20
  58.0 2.9 collective-permute-done.4
  60.9 6.9 %collective-permute-done.5 = f32[1,1,512,128]{3,2,1,0:T(8,128)S(1)} collective-permute-done((f32[1,1,512,128]{3,2,1,0:T(8,128)S(1)}, f32[1,1,512,128]{3,2,1,0:T(8,128)S(1)}, u32[]{:S(2)}, u32[]{:S(2)}) %collective-permute-start.5) | collective-permute-done | bytes 262176 | tf_op jit(solution)/shard_map/ppermute | solution.py:20
  73.7 6.3 %collective-permute-start.7 = (f32[1,1,512,128]{3,2,1,0:T(8,128)S(1)}, f32[1,1,512,128]{3,2,1,0:T(8,128)S(1)}, u32[]{:S(2)}, u32[]{:S(2)}) collective-permute-start(f32[1,1,512,128]{3,2,1,0:T(8,128)S(1)} %get-tuple-element.68), channel_id=1, source_target_pairs={{0,1},{1,2},{2,3},{3,4},{4,5},{5,6},{6,7},{7,8},{8,9},{9,10},{10,1... | collective-permute-start | bytes 786440 | tf_op jit(solution)/shard_map/ppermute | solution.py:20
  80.6 11.8 %gather_fusion.3 = f32[2048]{0:T(1024)S(1)} fusion(f32[131072]{0:T(1024)S(1)} %bitcast.103, s32[2048]{0:T(1024)S(1)} %broadcast_clamp_fusion), kind=kCustom, calls=%fused_computation.3.clone | custom fusion | bytes 24576 | tf_op jit(solution)/shard_map/jit(take_along_axis)/gather | solution.py:71
  92.4 11.8 %gather_fusion.2 = f32[2048]{0:T(1024)S(1)} fusion(f32[131072]{0:T(1024)S(1)} %bitcast.108, s32[2048]{0:T(1024)S(1)} %broadcast_clamp_fusion), kind=kCustom, calls=%fused_computation.2.clone | custom fusion | bytes 24576 | tf_op jit(solution)/shard_map/jit(take_along_axis)/gather | solution.py:71
  104.2 11.8 %gather_fusion.1 = f32[2048]{0:T(1024)S(1)} fusion(f32[131072]{0:T(1024)S(1)} %bitcast.113, s32[2048]{0:T(1024)S(1)} %broadcast_clamp_fusion), kind=kCustom, calls=%fused_computation.1.clone | custom fusion | bytes 24576 | tf_op jit(solution)/shard_map/jit(take_along_axis)/gather | solution.py:71
  119.8 11.8 %gather_fusion = f32[2048]{0:T(1024)S(1)} fusion(f32[131072]{0:T(1024)S(1)} %bitcast.119, s32[2048]{0:T(1024)S(1)} %broadcast_clamp_fusion), kind=kCustom, calls=%fused_computation.clone | custom fusion | bytes 24576 | tf_op jit(solution)/shard_map/jit(take_along_axis)/gather | solution.py:71
  131.7 14.0 %scatter_custom_fusion = f32[131072]{0:T(1024)S(1)} fusion(s32[2048]{0:T(1024)S(1)} %broadcast_select_fusion, f32[2048]{0:T(1024)S(1)} %bitcast.134, f32[]{:T(128)} %constant.123.clone.1), kind=kCustom, calls=%fused_computation.112 | custom fusion | flops 2048 | bytes 524292
  147.2 5.6 %collective-permute-start.9 = (f32[1,1,512,128]{3,2,1,0:T(8,128)S(1)}, f32[1,1,512,128]{3,2,1,0:T(8,128)S(1)}, u32[]{:S(2)}, u32[]{:S(2)}) collective-permute-start(f32[1,1,512,128]{3,2,1,0:T(8,128)S(1)} %get-tuple-element.66), channel_id=1, source_target_pairs={{0,1},{1,2},{2,3},{3,4},{4,5},{5,6},{6,7},{7,8},{8,9},{9,10},{10,1... | collective-permute-start | bytes 786440 | tf_op jit(solution)/shard_map/ppermute | solution.py:20
  152.8 3.6 collective-permute-done.8
  156.4 7.0 %collective-permute-done.9 = f32[1,1,512,128]{3,2,1,0:T(8,128)S(1)} collective-permute-done((f32[1,1,512,128]{3,2,1,0:T(8,128)S(1)}, f32[1,1,512,128]{3,2,1,0:T(8,128)S(1)}, u32[]{:S(2)}, u32[]{:S(2)}) %collective-permute-start.9) | collective-permute-done | bytes 262176 | tf_op jit(solution)/shard_map/ppermute | solution.py:20
  163.8 14.1 %scatter_fusion = f32[131072]{0:T(1024)S(1)} fusion(f32[131072]{0:T(1024)S(1)} %bitcast.87, s32[2048]{0:T(1024)S(1)} %broadcast_select_fusion, f32[2048]{0:T(1024)S(1)} %bitcast.128), kind=kCustom, calls=%fused_computation.5 | custom fusion | flops 2048 | bytes 32768
  179.3 5.5 %collective-permute-start.11 = (f32[1,1,512,128]{3,2,1,0:T(8,128)S(1)}, f32[1,1,512,128]{3,2,1,0:T(8,128)S(1)}, u32[]{:S(2)}, u32[]{:S(2)}) collective-permute-start(f32[1,1,512,128]{3,2,1,0:T(8,128)S(1)} %get-tuple-element.64), channel_id=1, source_target_pairs={{0,1},{1,2},{2,3},{3,4},{4,5},{5,6},{6,7},{7,8},{8,9},{9,10},{10,1... | collective-permute-start | bytes 786440 | tf_op jit(solution)/shard_map/ppermute | solution.py:20
  184.8 4.0 %collective-permute-done.10 = f32[1,1,512,128]{3,2,1,0:T(8,128)S(1)} collective-permute-done((f32[1,1,512,128]{3,2,1,0:T(8,128)S(1)}, f32[1,1,512,128]{3,2,1,0:T(8,128)S(1)}, u32[]{:S(2)}, u32[]{:S(2)}) %collective-permute-start.10) | collective-permute-done | bytes 262176 | tf_op jit(solution)/shard_map/ppermute | solution.py:22
  188.9 6.5 %collective-permute-done.11 = f32[1,1,512,128]{3,2,1,0:T(8,128)S(1)} collective-permute-done((f32[1,1,512,128]{3,2,1,0:T(8,128)S(1)}, f32[1,1,512,128]{3,2,1,0:T(8,128)S(1)}, u32[]{:S(2)}, u32[]{:S(2)}) %collective-permute-start.11) | collective-permute-done | bytes 262176 | tf_op jit(solution)/shard_map/ppermute | solution.py:20
  195.9 14.1 %scatter_fusion.1 = f32[131072]{0:T(1024)S(1)} fusion(f32[131072]{0:T(1024)S(1)} %bitcast.93, s32[2048]{0:T(1024)S(1)} %broadcast_select_fusion, f32[2048]{0:T(1024)S(1)} %bitcast.127), kind=kCustom, calls=%fused_computation.6 | custom fusion | flops 2048 | bytes 32768
  211.5 5.5 %collective-permute-start.13 = (f32[1,1,512,128]{3,2,1,0:T(8,128)S(1)}, f32[1,1,512,128]{3,2,1,0:T(8,128)S(1)}, u32[]{:S(2)}, u32[]{:S(2)}) collective-permute-start(f32[1,1,512,128]{3,2,1,0:T(8,128)S(1)} %get-tuple-element.62), channel_id=1, source_target_pairs={{0,1},{1,2},{2,3},{3,4},{4,5},{5,6},{6,7},{7,8},{8,9},{9,10},{10,1... | collective-permute-start | bytes 786440 | tf_op jit(solution)/shard_map/ppermute | solution.py:20
  217.0 4.0 %collective-permute-done.12 = f32[1,1,512,128]{3,2,1,0:T(8,128)S(1)} collective-permute-done((f32[1,1,512,128]{3,2,1,0:T(8,128)S(1)}, f32[1,1,512,128]{3,2,1,0:T(8,128)S(1)}, u32[]{:S(2)}, u32[]{:S(2)}) %collective-permute-start.12) | collective-permute-done | bytes 262176 | tf_op jit(solution)/shard_map/ppermute | solution.py:22
  221.0 6.5 %collective-permute-done.13 = f32[1,1,512,128]{3,2,1,0:T(8,128)S(1)} collective-permute-done((f32[1,1,512,128]{3,2,1,0:T(8,128)S(1)}, f32[1,1,512,128]{3,2,1,0:T(8,128)S(1)}, u32[]{:S(2)}, u32[]{:S(2)}) %collective-permute-start.13) | collective-permute-done | bytes 262176 | tf_op jit(solution)/shard_map/ppermute | solution.py:20
  228.1 14.1 %scatter_fusion.2 = f32[131072]{0:T(1024)S(1)} fusion(f32[131072]{0:T(1024)S(1)} %bitcast.115, s32[2048]{0:T(1024)S(1)} %broadcast_select_fusion, f32[2048]{0:T(1024)S(1)} %bitcast.126), kind=kCustom, calls=%fused_computation.7 | custom fusion | flops 2048 | bytes 32768
  242.2 2.4 add_bitcast_fusion
  246.0 5.5 %collective-permute-start.15 = (f32[1,18,128]{2,1,0:T(8,128)S(1)}, f32[1,18,128]{2,1,0:T(8,128)S(1)}, u32[]{:S(2)}, u32[]{:S(2)}) collective-permute-start(f32[1,18,128]{2,1,0:T(8,128)S(1)} %get-tuple-element.60), channel_id=1, source_target_pairs={{0,1},{1,2},{2,3},{3,4},{4,5},{5,6},{6,7},{7,8},{8,9},{9,10},{10,1... | collective-permute-start | bytes 27656 | tf_op jit(solution)/shard_map/ppermute | solution.py:20
  252.3 113.6 %reduce-scatter.2.cloned.1.call-done = f32[2,16,128]{2,1,0:T(8,128)} async-done(((f32[2,512,128]{2,1,0:T(8,128)}), f32[2,16,128]{2,1,0:T(8,128)}) %reduce-scatter.2.cloned.1.call-update) | async-done | bytes 16400 | tf_op jit(solution)/shard_map/reduce_scatter | solution.py:86
  365.9 1.4 fusion.61
  (66 shorter events, 21.8 us)
Async XLA Ops:
  7.2 16.9 %copy-start.2 = (f32[1,2,512,128]{3,2,1,0:T(8,128)S(1)}, f32[1,2,512,128]{3,2,1,0:T(8,128)}, u32[]{:S(2)}) copy-start(f32[1,2,512,128]{3,2,1,0:T(8,128)} %param.18) | copy-start | bytes 1572868
  7.2 9.3 %copy-start.5 = (f32[1,4]{1,0:T(1,128)S(1)}, f32[1,4]{1,0:T(1,128)}, u32[]{:S(2)}) copy-start(f32[1,4]{1,0:T(1,128)} %param.20) | copy-start | bytes 52
  7.2 12.0 %copy-start.3 = (s32[1,2048]{1,0:T(1,128)S(1)}, s32[1,2048]{1,0:T(1,128)}, u32[]{:S(2)}) copy-start(s32[1,2048]{1,0:T(1,128)} %param.22) | copy-start | bytes 24580
  7.2 16.8 %copy-start.1 = (f32[2,512,128]{2,1,0:T(8,128)S(1)}, f32[2,512,128]{2,1,0:T(8,128)}, u32[]{:S(2)}) copy-start(f32[2,512,128]{2,1,0:T(8,128)} %param.17) | copy-start | bytes 1572868
  7.2 358.7 %reduce-scatter.2.cloned.1.call-start = ((), (), s32[]{:S(2)}) async-start(), calls=%async_computation.1 | async-start | bytes 540672 | tf_op jit(solution)/shard_map/reduce_scatter | solution.py:86
  8.4 10.9 %collective-permute-start = (f32[1,1,512,128]{3,2,1,0:T(8,128)S(1)}, f32[1,1,512,128]{3,2,1,0:T(8,128)S(1)}, u32[]{:S(2)}, u32[]{:S(2)}) collective-permute-start(f32[1,1,512,128]{3,2,1,0:T(8,128)S(1)} %get-tuple-element.73), channel_id=1, source_target_pairs={{1,0},{2,1},{3,2},{4,3},{5,4},{6,5},{7,6},{8,7},{9,8},{10,9},{11,1... | collective-permute-start | bytes 786440 | tf_op jit(solution)/shard_map/ppermute | solution.py:22
  9.7 14.3 %collective-permute-start.1 = (f32[1,1,512,128]{3,2,1,0:T(8,128)S(1)}, f32[1,1,512,128]{3,2,1,0:T(8,128)S(1)}, u32[]{:S(2)}, u32[]{:S(2)}) collective-permute-start(f32[1,1,512,128]{3,2,1,0:T(8,128)S(1)} %get-tuple-element.74), channel_id=1, source_target_pairs={{0,1},{1,2},{2,3},{3,4},{4,5},{5,6},{6,7},{7,8},{8,9},{9,10},{10,1... | collective-permute-start | bytes 786440 | tf_op jit(solution)/shard_map/ppermute | solution.py:20
  28.1 9.4 %collective-permute-start.2 = (f32[1,1,512,128]{3,2,1,0:T(8,128)S(1)}, f32[1,1,512,128]{3,2,1,0:T(8,128)S(1)}, u32[]{:S(2)}, u32[]{:S(2)}) collective-permute-start(f32[1,1,512,128]{3,2,1,0:T(8,128)S(1)} %get-tuple-element.71), channel_id=1, source_target_pairs={{1,0},{2,1},{3,2},{4,3},{5,4},{6,5},{7,6},{8,7},{9,8},{10,9},{11,1... | collective-permute-start | bytes 786440 | tf_op jit(solution)/shard_map/ppermute | solution.py:22
  29.4 16.3 %collective-permute-start.3 = (f32[1,1,512,128]{3,2,1,0:T(8,128)S(1)}, f32[1,1,512,128]{3,2,1,0:T(8,128)S(1)}, u32[]{:S(2)}, u32[]{:S(2)}) collective-permute-start(f32[1,1,512,128]{3,2,1,0:T(8,128)S(1)} %get-tuple-element.72), channel_id=1, source_target_pairs={{0,1},{1,2},{2,3},{3,4},{4,5},{5,6},{6,7},{7,8},{8,9},{9,10},{10,1... | collective-permute-start | bytes 786440 | tf_op jit(solution)/shard_map/ppermute | solution.py:20
  49.6 7.6 %copy-start.7 = (s32[2]{0:T(128)S(1)}, s32[2]{0:T(128)}, u32[]{:S(2)}) copy-start(s32[2]{0:T(128)} %constant.172) | copy-start | bytes 28
  49.6 11.3 %collective-permute-start.4 = (f32[1,1,512,128]{3,2,1,0:T(8,128)S(1)}, f32[1,1,512,128]{3,2,1,0:T(8,128)S(1)}, u32[]{:S(2)}, u32[]{:S(2)}) collective-permute-start(f32[1,1,512,128]{3,2,1,0:T(8,128)S(1)} %get-tuple-element.69), channel_id=1, source_target_pairs={{1,0},{2,1},{3,2},{4,3},{5,4},{6,5},{7,6},{8,7},{9,8},{10,9},{11,1... | collective-permute-start | bytes 786440 | tf_op jit(solution)/shard_map/ppermute | solution.py:22
  50.9 16.8 %collective-permute-start.5 = (f32[1,1,512,128]{3,2,1,0:T(8,128)S(1)}, f32[1,1,512,128]{3,2,1,0:T(8,128)S(1)}, u32[]{:S(2)}, u32[]{:S(2)}) collective-permute-start(f32[1,1,512,128]{3,2,1,0:T(8,128)S(1)} %get-tuple-element.70), channel_id=1, source_target_pairs={{0,1},{1,2},{2,3},{3,4},{4,5},{5,6},{6,7},{7,8},{8,9},{9,10},{10,1... | collective-permute-start | bytes 786440 | tf_op jit(solution)/shard_map/ppermute | solution.py:20
  71.6 8.3 %copy-start.6 = (s32[2]{0:T(128)S(1)}, s32[2]{0:T(128)}, u32[]{:S(2)}) copy-start(s32[2]{0:T(128)} %constant.169) | copy-start | bytes 28
  72.4 43.6 %collective-permute-start.6 = (f32[1,1,512,128]{3,2,1,0:T(8,128)}, f32[1,1,512,128]{3,2,1,0:T(8,128)S(1)}, u32[]{:S(2)}, u32[]{:S(2)}) collective-permute-start(f32[1,1,512,128]{3,2,1,0:T(8,128)} %get-tuple-element.67), channel_id=1, source_target_pairs={{1,0},{2,1},{3,2},{4,3},{5,4},{6,5},{7,6},{8,7},{9,8},{10,9},{11,1... | collective-permute-start | bytes 786440 | tf_op jit(solution)/shard_map/ppermute | solution.py:22
  73.7 42.3 %collective-permute-start.7 = (f32[1,1,512,128]{3,2,1,0:T(8,128)S(1)}, f32[1,1,512,128]{3,2,1,0:T(8,128)S(1)}, u32[]{:S(2)}, u32[]{:S(2)}) collective-permute-start(f32[1,1,512,128]{3,2,1,0:T(8,128)S(1)} %get-tuple-element.68), channel_id=1, source_target_pairs={{0,1},{1,2},{2,3},{3,4},{4,5},{5,6},{6,7},{7,8},{8,9},{9,10},{10,1... | collective-permute-start | bytes 786440 | tf_op jit(solution)/shard_map/ppermute | solution.py:20
  119.8 11.8 %copy-start = (f32[1,131072]{1,0:T(1,128)}, f32[1,131072]{1,0:T(1,128)S(1)}, u32[]{:S(2)}) copy-start(f32[1,131072]{1,0:T(1,128)S(1)} %scatter-add.51) | copy-start | bytes 1572868
  119.8 11.8 %copy-start.4 = (f32[1,4,2048]{2,1,0:T(4,128)S(1)}, f32[1,4,2048]{2,1,0:T(4,128)}, u32[]{:S(2)}) copy-start(f32[1,4,2048]{2,1,0:T(4,128)} %param.23) | copy-start | bytes 98308
  145.9 10.5 %collective-permute-start.8 = (f32[1,1,512,128]{3,2,1,0:T(8,128)S(1)}, f32[1,1,512,128]{3,2,1,0:T(8,128)S(1)}, u32[]{:S(2)}, u32[]{:S(2)}) collective-permute-start(f32[1,1,512,128]{3,2,1,0:T(8,128)S(1)} %get-tuple-element.65), channel_id=1, source_target_pairs={{1,0},{2,1},{3,2},{4,3},{5,4},{6,5},{7,6},{8,7},{9,8},{10,9},{11,1... | collective-permute-start | bytes 786440 | tf_op jit(solution)/shard_map/ppermute | solution.py:22
  147.2 16.2 %collective-permute-start.9 = (f32[1,1,512,128]{3,2,1,0:T(8,128)S(1)}, f32[1,1,512,128]{3,2,1,0:T(8,128)S(1)}, u32[]{:S(2)}, u32[]{:S(2)}) collective-permute-start(f32[1,1,512,128]{3,2,1,0:T(8,128)S(1)} %get-tuple-element.66), channel_id=1, source_target_pairs={{0,1},{1,2},{2,3},{3,4},{4,5},{5,6},{6,7},{7,8},{8,9},{9,10},{10,1... | collective-permute-start | bytes 786440 | tf_op jit(solution)/shard_map/ppermute | solution.py:20
  178.0 10.9 %collective-permute-start.10 = (f32[1,1,512,128]{3,2,1,0:T(8,128)S(1)}, f32[1,1,512,128]{3,2,1,0:T(8,128)S(1)}, u32[]{:S(2)}, u32[]{:S(2)}) collective-permute-start(f32[1,1,512,128]{3,2,1,0:T(8,128)S(1)} %get-tuple-element.63), channel_id=1, source_target_pairs={{1,0},{2,1},{3,2},{4,3},{5,4},{6,5},{7,6},{8,7},{9,8},{10,9},{11,1... | collective-permute-start | bytes 786440 | tf_op jit(solution)/shard_map/ppermute | solution.py:22
  179.3 16.1 %collective-permute-start.11 = (f32[1,1,512,128]{3,2,1,0:T(8,128)S(1)}, f32[1,1,512,128]{3,2,1,0:T(8,128)S(1)}, u32[]{:S(2)}, u32[]{:S(2)}) collective-permute-start(f32[1,1,512,128]{3,2,1,0:T(8,128)S(1)} %get-tuple-element.64), channel_id=1, source_target_pairs={{0,1},{1,2},{2,3},{3,4},{4,5},{5,6},{6,7},{7,8},{8,9},{9,10},{10,1... | collective-permute-start | bytes 786440 | tf_op jit(solution)/shard_map/ppermute | solution.py:20
  210.2 10.9 %collective-permute-start.12 = (f32[1,1,512,128]{3,2,1,0:T(8,128)S(1)}, f32[1,1,512,128]{3,2,1,0:T(8,128)S(1)}, u32[]{:S(2)}, u32[]{:S(2)}) collective-permute-start(f32[1,1,512,128]{3,2,1,0:T(8,128)S(1)} %get-tuple-element.61), channel_id=1, source_target_pairs={{1,0},{2,1},{3,2},{4,3},{5,4},{6,5},{7,6},{8,7},{9,8},{10,9},{11,1... | collective-permute-start | bytes 786440 | tf_op jit(solution)/shard_map/ppermute | solution.py:22
  211.5 16.1 %collective-permute-start.13 = (f32[1,1,512,128]{3,2,1,0:T(8,128)S(1)}, f32[1,1,512,128]{3,2,1,0:T(8,128)S(1)}, u32[]{:S(2)}, u32[]{:S(2)}) collective-permute-start(f32[1,1,512,128]{3,2,1,0:T(8,128)S(1)} %get-tuple-element.62), channel_id=1, source_target_pairs={{0,1},{1,2},{2,3},{3,4},{4,5},{5,6},{6,7},{7,8},{8,9},{9,10},{10,1... | collective-permute-start | bytes 786440 | tf_op jit(solution)/shard_map/ppermute | solution.py:20
  244.7 6.9 %collective-permute-start.14 = (f32[1,18,128]{2,1,0:T(8,128)S(1)}, f32[1,18,128]{2,1,0:T(8,128)S(1)}, u32[]{:S(2)}, u32[]{:S(2)}) collective-permute-start(f32[1,18,128]{2,1,0:T(8,128)S(1)} %get-tuple-element.59), channel_id=1, source_target_pairs={{1,0},{2,1},{3,2},{4,3},{5,4},{6,5},{7,6},{8,7},{9,8},{10,9},{11,1... | collective-permute-start | bytes 27656 | tf_op jit(solution)/shard_map/ppermute | solution.py:22
  246.0 6.3 %collective-permute-start.15 = (f32[1,18,128]{2,1,0:T(8,128)S(1)}, f32[1,18,128]{2,1,0:T(8,128)S(1)}, u32[]{:S(2)}, u32[]{:S(2)}) collective-permute-start(f32[1,18,128]{2,1,0:T(8,128)S(1)} %get-tuple-element.60), channel_id=1, source_target_pairs={{0,1},{1,2},{2,3},{3,4},{4,5},{5,6},{6,7},{7,8},{8,9},{9,10},{10,1... | collective-permute-start | bytes 27656 | tf_op jit(solution)/shard_map/ppermute | solution.py:20
Sparse Core Ops, SparseCore 0:
  244.7 121.0 reduce-scatter.1
where the time goes:
time: 377 us; the launch traced here: 374 us
  waiting for transfers between devices  171 us (45%)
  other arithmetic  70.3 us (19%)
  starting transfers between devices  57.4 us (15%)
  local copies, waits for them, and re-layouts  50.4 us (13%)
  between operations  25.4 us (7%)
    reduce_scatter x1, waiting for transfers between devices, shards(): owned = lax.psum_scatter(image, 'shot', scatter_dimension=1, tiled=True)  114 us
    unnamed x7, other arithmetic  56.7 us
    gather x4, local copies, waits for them, and re-layouts, shards(): taken = jnp.take_along_axis(misfit_flat, receiver_at, axis=1)  47.1 us
    ppermute x8, starting transfers between devices, with_halo(): lax.ppermute(tail, axis, [(i, (i + 1) % count) for i in range(ends)])  47 us
    ppermute x8, waiting for transfers between devices, with_halo(): lax.ppermute(tail, axis, [(i, (i + 1) % count) for i in range(ends)])  40.7 us
    ppermute x8, waiting for transfers between devices, with_halo(): lax.ppermute(head, axis, [((i + 1) % count, i) for i in range(ends)])  16.4 us
    ppermute x8, starting transfers between devices, with_halo(): lax.ppermute(head, axis, [((i + 1) % count, i) for i in range(ends)])  10.3 us
  transfers between devices with their start and end apart: 17, of which 13 were waited for; matrix products, arithmetic and copies ran while one was open for 10% of the time, Pallas kernels for 0%

commit v1 on v0

v1 whole, which is shorter than its diff:
```python
import jax
import jax.numpy as jnp
from jax import lax
from jax.experimental import pallas as pl
from jax.experimental.pallas import tpu as pltpu
from jax.sharding import PartitionSpec as P


NT = 4
PRIOR_GAIN = 50.0
PLANES = 4
ROWS = 264
SHIFT = 248
PAD = 8
BLOCK = 24
CHUNKS = ((0, 96), (96, 96), (192, 72))
CELL_ROWS = PLANES * ROWS
TILE = 352
COLUMNS = 9 * 128
MESH = pl.DeviceIdType.MESH


def kernel(
    kappa_ref, now_ref, before_ref, wavelet_ref, source_ref, receiver_ref, observed_ref,
    gradient_ref, next_ref,
    u, model, source, laps, counts, adjoint, weighted, halo, image,
    onehot_rows, onehot_lanes, kappa_rows, kappa_rim, mate, summed, landed,
    local_sem, pair_send, pair_recv, rim_send, rim_recv, halo_send, halo_recv,
    next_sem, core_send, core_recv, band_send, band_recv,
):
    shot = lax.axis_index("shot")
    dom = lax.axis_index("dom")
    h = lax.rem(dom, 2)
    slab = dom // 2
    core = lax.rem(shot, 2)
    x_lo = lax.rem(shot // 2, 2)
    z = shot // 4
    pair = (shot, dom + 1 - 2 * h)
    above = (shot, lax.rem(dom + 2, 16))
    below = (shot, lax.rem(dom + 14, 16))
    next_dom = (shot, lax.rem(dom + 1, 16))
    last_dom = (shot, lax.rem(dom + 15, 16))
    other = (shot, lax.rem(dom + 15 + 2 * h, 16))
    twin = (shot + 1 - 2 * core, dom)
    in_half = z // 4 == h
    has_below = slab > 0
    has_above = slab < 7

    def copy_to(device, src, dst, send, recv):
        return pltpu.make_async_remote_copy(
            src_ref=src, dst_ref=dst, send_sem=send, recv_sem=recv, device_id=device, device_id_type=MESH
        )

    def owner(j):
        brick, lo, quarter = j // 8, lax.rem(j // 4, 2), lax.rem(j, 4)
        mine = (brick == h) & (lo == x_lo) & (4 * h + quarter == z)
        return brick, lo, quarter, mine, ((4 * h + quarter) * 4 + lo * 2 + core, 2 * slab + brick)

    def giver(j):
        mine = in_half & (j == z * 2 + x_lo)
        return mine, (j * 2 + core, 2 * slab + z // 4)

    mine_rows = pl.ds(pl.multiple_of(h * SHIFT, 8), ROWS)
    pair_rows = pl.ds(pl.multiple_of((1 - h) * SHIFT, 8), ROWS)
    own = pl.ds(2 * h, 2)
    theirs = pl.ds(2 - 2 * h, 2)
    body = pl.ds(PAD, ROWS)

    loads = [
        pltpu.make_async_copy(now_ref.at[0, :, mine_rows], u.at[1, own, body], local_sem.at[0]),
        pltpu.make_async_copy(kappa_ref.at[:, mine_rows], model.at[own], local_sem.at[1]),
        pltpu.make_async_copy(before_ref.at[0, :, mine_rows], u.at[0, own, body], local_sem.at[2]),
        pltpu.make_async_copy(kappa_ref, kappa_rows.at[:, pl.ds(PAD, 512)], local_sem.at[3]),
    ]
    for load in loads:
        load.start()

    barrier = pltpu.get_barrier_semaphore()
    for device in (pair, above, below, other, twin):
        pl.semaphore_signal(barrier, inc=1, device_id=device, device_id_type=MESH)

    def greet(j, carry):
        _, _, _, mine, device = owner(j)

        @pl.when(jnp.logical_not(mine))
        def _():
            pl.semaphore_signal(barrier, inc=1, device_id=device, device_id_type=MESH)

        mine_too, device_too = giver(j)

        @pl.when(jnp.logical_not(mine_too))
        def _():
            pl.semaphore_signal(barrier, inc=1, device_id=device_too, device_id_type=MESH)

        return carry

    lax.fori_loop(0, 16, greet, 0)
    pl.semaphore_wait(barrier, 37 - 2 * in_half.astype(jnp.int32))

    exchange = [
        copy_to(pair, now_ref.at[0, :, pair_rows], u.at[1, own, body], pair_send.at[0], pair_recv.at[0]),
        copy_to(pair, kappa_ref.at[:, pair_rows], model.at[own], pair_send.at[1], pair_recv.at[1]),
        copy_to(pair, before_ref.at[0, :, pair_rows], u.at[0, own, body], pair_send.at[2], pair_recv.at[2]),
    ]
    for copy in exchange:
        copy.start()
    band_rows = pl.ds(pl.multiple_of(shot * 16, 8), 16)
    rims = [
        copy_to(next_dom, kappa_ref.at[1, band_rows], kappa_rim.at[0], rim_send.at[0], rim_recv.at[0]),
        copy_to(last_dom, kappa_ref.at[0, band_rows], kappa_rim.at[1], rim_send.at[1], rim_recv.at[1]),
    ]
    for copy in rims:
        copy.start()

    for n in range(6):
        for p in range(PLANES):
            u[n, p, 0:PAD] = jnp.zeros((PAD, 128), jnp.float32)
            u[n, p, PAD + ROWS : 2 * PAD + ROWS] = jnp.zeros((PAD, 128), jnp.float32)
    for n in range(3):
        for p in range(PLANES):
            weighted[n, p, 0:PAD] = jnp.zeros((PAD, 128), jnp.float32)
            weighted[n, p, PAD + ROWS : 2 * PAD + ROWS] = jnp.zeros((PAD, 128), jnp.float32)
    for p in range(2):
        kappa_rows[p, 0:PAD] = jnp.zeros((PAD, 128), jnp.float32)
        kappa_rows[p, PAD + 512 : 2 * PAD + 512] = jnp.zeros((PAD, 128), jnp.float32)

    cell = receiver_ref[...]
    plane = lax.shift_right_logical(cell, 16) - PLANES * slab
    row = lax.bitwise_and(lax.shift_right_logical(cell, 7), 511) - SHIFT * h
    inside = (plane >= 0) & (plane < PLANES) & (row >= 0) & (row < ROWS)
    cell_row = jnp.where(inside, plane * ROWS + row, -1)
    lane = lax.bitwise_and(cell, 127)

    def fill_rows(i, carry):
        start = pl.multiple_of(i * 16, 16)
        ids = lax.broadcasted_iota(jnp.int32, (16, 2048), 0) + start
        onehot_rows[pl.ds(start, 16)] = jnp.where(ids == cell_row, 1.0, 0.0).astype(jnp.bfloat16)
        return carry

    lax.fori_loop(0, CELL_ROWS // 16, fill_rows, 0)

    values = observed_ref[0]
    high = values.astype(jnp.bfloat16).astype(jnp.float32)
    low = values - high

    def fill_lanes(i, carry):
        start = pl.multiple_of(i * 16, 16)
        hit = lax.broadcasted_iota(jnp.int32, (16, 2048), 0) + start == lane
        onehot_lanes[pl.ds(start, 16)] = jnp.where(hit, 1.0, 0.0).astype(jnp.bfloat16)
        for n in range(NT):
            onehot_lanes[pl.ds(128 * (1 + n) + start, 16)] = jnp.where(hit, high[n : n + 1], 0.0).astype(jnp.bfloat16)
            onehot_lanes[pl.ds(128 * (5 + n) + start, 16)] = jnp.where(hit, low[n : n + 1], 0.0).astype(jnp.bfloat16)
        return carry

    lax.fori_loop(0, 8, fill_lanes, 0)

    def spread(i, carry):
        start = pl.multiple_of(i * TILE, 16)
        product = lax.dot_general(
            onehot_rows[pl.ds(start, TILE)], onehot_lanes[...], (((1,), (1,)), ((), ())),
            preferred_element_type=jnp.float32,
        )
        counts[0, pl.ds(start, TILE)] = product[:, 0:128]
        for n in range(NT):
            counts[1 + n, pl.ds(start, TILE)] = (
                product[:, 128 * (1 + n) : 128 * (2 + n)] + product[:, 128 * (5 + n) : 128 * (6 + n)]
            )
        return carry

    lax.fori_loop(0, CELL_ROWS // TILE, spread, 0)

    spot = source_ref[0]
    spot_plane = lax.shift_right_logical(spot, 16) - PLANES * slab
    spot_row = lax.bitwise_and(lax.shift_right_logical(spot, 7), 511) - SHIFT * h
    spot_lane = lax.bitwise_and(spot, 127)
    lanes = lax.broadcasted_iota(jnp.int32, (BLOCK, 128), 1)
    block_rows = lax.broadcasted_iota(jnp.int32, (BLOCK, 128), 0)
    first_lane = lanes == 0
    last_lane = lanes == 127

    def laplace(field, rim, p, r):
        middle = field[p, pl.ds(PAD + r, BLOCK)]
        if p < PLANES - 1:
            after = field[p + 1, pl.ds(PAD + r, BLOCK)]
        else:
            after = jnp.where(has_above, rim[1, pl.ds(r, BLOCK)], 0.0)
        if p > 0:
            prior = field[p - 1, pl.ds(PAD + r, BLOCK)]
        else:
            prior = jnp.where(has_below, rim[0, pl.ds(r, BLOCK)], 0.0)
        total = after + prior
        total = total + field[p, pl.ds(PAD + 1 + r, BLOCK)] + field[p, pl.ds(PAD - 1 + r, BLOCK)]
        total = total + jnp.where(last_lane, 0.0, pltpu.roll(middle, 127, 1))
        total = total + jnp.where(first_lane, 0.0, pltpu.roll(middle, 1, 1))
        return total - 6.0 * middle, middle

    def forward(n, planes, first, size):
        def block(i, carry):
            r = pl.multiple_of(first + i * BLOCK, 8)
            for p in planes:
                lap, middle = laplace(u.at[n + 1], halo.at[n], p, r)
                speed = model[p, pl.ds(r, BLOCK)]
                pulse = jnp.where(
                    (spot_plane == p) & (spot_lane == lanes) & (spot_row - r == block_rows), wavelet_ref[0, n], 0.0
                )
                after = 2.0 * middle - u[n, p, pl.ds(PAD + r, BLOCK)] + speed * lap + pulse
                u[n + 2, p, pl.ds(PAD + r, BLOCK)] = after
                if n < NT - 1:
                    laps[n, p, pl.ds(r, BLOCK)] = lap
                else:
                    miss = counts[0, pl.ds(p * ROWS + r, BLOCK)] * after - counts[NT, pl.ds(p * ROWS + r, BLOCK)]
                    adjoint[0, p, pl.ds(r, BLOCK)] = miss
                    weighted[0, p, pl.ds(PAD + r, BLOCK)] = speed * miss
                    image[p, pl.ds(r, BLOCK)] = miss * lap
            return carry

        lax.fori_loop(0, size // BLOCK, block, 0)

    def backward(j, planes, first, size):
        level = NT - 1 - j

        def block(i, carry):
            r = pl.multiple_of(first + i * BLOCK, 8)
            for p in planes:
                lap, _ = laplace(weighted.at[j], halo.at[NT + j], p, r)
                at = pl.ds(p * ROWS + r, BLOCK)
                miss = counts[0, at] * u[level + 1, p, pl.ds(PAD + r, BLOCK)] - counts[level, at]
                field = 2.0 * adjoint[j, p, pl.ds(r, BLOCK)] + lap + miss
                if j > 0:
                    field = field - adjoint[j - 1, p, pl.ds(r, BLOCK)]
                image[p, pl.ds(r, BLOCK)] += field * laps[level - 1, p, pl.ds(r, BLOCK)]
                if level > 1:
                    adjoint[j + 1, p, pl.ds(r, BLOCK)] = field
                    weighted[j + 1, p, pl.ds(PAD + r, BLOCK)] = model[p, pl.ds(r, BLOCK)] * field
            return carry

        lax.fori_loop(0, size // BLOCK, block, 0)

    def rim_copies(field, n, c):
        first, size = CHUNKS[c]
        at, to = pl.ds(PAD + first, size), pl.ds(first, size)
        return (
            copy_to(above, field.at[PLANES - 1, at], halo.at[n, 0, to], halo_send.at[n, c, 0], halo_recv.at[n, c, 0]),
            copy_to(below, field.at[0, at], halo.at[n, 1, to], halo_send.at[n, c, 1], halo_recv.at[n, c, 1]),
        )

    halos = []

    def send_rims(field, n, c):
        for copy in rim_copies(field, n, c):
            copy.start()
            halos.append(copy)

    loads[0].wait()
    exchange[0].wait_recv()
    for c in range(len(CHUNKS)):
        send_rims(u.at[1], 0, c)
    for load in loads[1:]:
        load.wait()
    exchange[1].wait_recv()
    exchange[2].wait_recv()

    for n in range(NT):
        forward(n, (1, 2), 0, ROWS)
        for c, (first, size) in enumerate(CHUNKS):
            for copy in rim_copies(u.at[n + 1], n, c):
                copy.wait_recv()
            forward(n, (0, 3), first, size)
            if n < NT - 1:
                send_rims(u.at[n + 2], n + 1, c)
            else:
                send_rims(weighted.at[0], NT, c)

    half = pl.ds(pl.multiple_of(h * 256, 8), 256)
    kept = pl.ds(pl.multiple_of(PAD + 8 * h, 8), 256)
    store = pltpu.make_async_copy(u.at[NT + 1, own, kept], next_ref.at[0, :, half], next_sem.at[0])
    give = copy_to(pair, u.at[NT + 1, theirs, kept], next_ref.at[0, :, half], next_sem.at[1], next_sem.at[2])
    store.start()
    give.start()

    for j in range(NT - 1):
        backward(j, (1, 2), 0, ROWS)
        for c, (first, size) in enumerate(CHUNKS):
            for copy in rim_copies(weighted.at[j], NT + j, c):
                copy.wait_recv()
            backward(j, (0, 3), first, size)
            if j < NT - 2:
                send_rims(weighted.at[j + 1], NT + j + 1, c)

    def band(j, parity):
        return pl.ds(pl.multiple_of(8 * h + 16 * (2 * j + parity), 8), 16)

    def core_copy(j):
        return copy_to(twin, image.at[:, band(j, 1 - core)], mate.at[j], core_send.at[j], core_recv.at[j])

    def core_start(j, carry):
        core_copy(j).start()
        return carry

    def core_sum(j, carry):
        core_copy(j).wait_recv()
        summed[j] = image[:, band(j, core)] + mate[j]
        return carry

    lax.fori_loop(0, 8, core_start, 0)
    lax.fori_loop(0, 8, core_sum, 0)

    slot = z * 2 + x_lo

    def band_copy(j):
        brick, lo, quarter, mine, device = owner(j)
        src = summed.at[quarter * 2 + lo, pl.ds(2 * brick, 2)]
        return mine, copy_to(device, src, landed.at[slot], band_send.at[j], band_recv.at[slot])

    def band_start(j, carry):
        mine, copy = band_copy(j)

        @pl.when(jnp.logical_not(mine))
        def _():
            copy.start()

        return carry

    lax.fori_loop(0, 16, band_start, 0)

    @pl.when(in_half)
    def _():
        landed[slot] = summed[(z - 4 * h) * 2 + x_lo, pl.ds(2 * h, 2)]

    for copy in rims:
        copy.wait_recv()

    band_lanes = lax.broadcasted_iota(jnp.int32, (16, 128), 1)
    start = pl.multiple_of(PAD + shot * 16, 8)
    for p in range(2):
        middle = kappa_rows[p, pl.ds(start, 16)]
        if p == 0:
            after = kappa_rows[1, pl.ds(start, 16)]
            prior = jnp.where(dom > 0, kappa_rim[0], 0.0)
        else:
            after = jnp.where(dom < 15, kappa_rim[1], 0.0)
            prior = kappa_rows[0, pl.ds(start, 16)]
        total = after + prior
        total = total + kappa_rows[p, pl.ds(start + 1, 16)] + kappa_rows[p, pl.ds(start - 1, 16)]
        total = total + jnp.where(band_lanes == 127, 0.0, pltpu.roll(middle, 127, 1))
        total = total + jnp.where(band_lanes == 0, 0.0, pltpu.roll(middle, 1, 1))
        gradient_ref[p] = (total / 6.0 - middle) * PRIOR_GAIN

    def band_wait(j, carry):
        mine, _ = giver(j)

        @pl.when(jnp.logical_not(mine))
        def _():
            copy_to(twin, landed.at[j], landed.at[j], band_send.at[j], band_recv.at[j]).wait_recv()

        return carry

    lax.fori_loop(0, 16, band_wait, 0)
    total = landed[0]
    for j in range(1, 16):
        total = total + landed[j]
    gradient_ref[...] = total / NT - gradient_ref[...]

    def band_done(j, carry):
        mine, copy = band_copy(j)

        @pl.when(jnp.logical_not(mine))
        def _():
            copy.wait_send()

        return carry

    def core_done(j, carry):
        core_copy(j).wait_send()
        return carry

    store.wait()
    give.wait()
    for copy in exchange + rims + halos:
        copy.wait_send()
    lax.fori_loop(0, 8, core_done, 0)
    lax.fori_loop(0, 16, band_done, 0)


def shards(kappa, wave_now, wave_before, wavelet, source_cell, receiver_cells, observed):
    f32 = jnp.float32
    chunks = len(CHUNKS)
    anywhere = pl.BlockSpec(memory_space=pl.ANY)
    vmem = pl.BlockSpec(memory_space=pltpu.VMEM)
    smem = pl.BlockSpec(memory_space=pltpu.SMEM)
    dma = pltpu.SemaphoreType.DMA
    return pl.pallas_call(
        kernel,
        out_shape=(
            jax.ShapeDtypeStruct((2, 16, 128), f32),
            jax.ShapeDtypeStruct(wave_now.shape, f32),
        ),
        in_specs=[anywhere, anywhere, anywhere, smem, smem, vmem, vmem],
        out_specs=(vmem, anywhere),
        scratch_shapes=[
            pltpu.VMEM((6, PLANES, ROWS + 2 * PAD, 128), f32),
            pltpu.VMEM((PLANES, ROWS, 128), f32),
            pltpu.VMEM((8, 128), f32),
            pltpu.VMEM((3, PLANES, ROWS, 128), f32),
            pltpu.VMEM((5, CELL_ROWS, 128), f32),
            pltpu.VMEM((3, PLANES, ROWS, 128), f32),
            pltpu.VMEM((3, PLANES, ROWS + 2 * PAD, 128), f32),
            pltpu.VMEM((7, 2, ROWS, 128), f32),
            pltpu.VMEM((PLANES, ROWS, 128), f32),
            pltpu.VMEM((CELL_ROWS, 2048), jnp.bfloat16),
            pltpu.VMEM((COLUMNS, 2048), jnp.bfloat16),
            pltpu.VMEM((2, 512 + 2 * PAD, 128), f32),
            pltpu.VMEM((2, 16, 128), f32),
            pltpu.VMEM((8, PLANES, 16, 128), f32),
            pltpu.VMEM((8, PLANES, 16, 128), f32),
            pltpu.VMEM((16, 2, 16, 128), f32),
            dma((4,)),
            dma((3,)),
            dma((3,)),
            dma((2,)),
            dma((2,)),
            dma((7, chunks, 2)),
            dma((7, chunks, 2)),
            dma((3,)),
            dma((8,)),
            dma((8,)),
            dma((16,)),
            dma((16,)),
        ],
        name="window",
        compiler_params=pltpu.CompilerParams(
            collective_id=0, has_side_effects=True, vmem_limit_bytes=56 << 20
        ),
    )(kappa, wave_now, wave_before, wavelet, source_cell, receiver_cells, observed)


def solution(mesh):
    return jax.shard_map(
        shards,
        mesh=mesh,
        in_specs=(
            P("dom", None, None),
            P("shot", "dom", None, None),
            P("shot", "dom", None, None),
            P("shot", None),
            P("shot"),
            P("shot", None),
            P("shot", None, None),
        ),
        out_specs=(P("dom", "shot", None), P("shot", "dom", None, None)),
        check_vma=False,
    )
```

time: 377 us -> 83.7 us (0.22)
  the two profiles are of different devices: /device:TPU:1 before, /device:TPU:71 now
where the time goes in v1:
time: 83.7 us; the launch traced here: 83.4 us
  Pallas kernels  78.9 us (94%)
  local copies, waits for them, and re-layouts  3.19 us (4%)
  between operations  1.29 us (2%)
    pallas_call x1, Pallas kernels, shards(): pl.pallas_call(kernel, out_shape=(jax.ShapeDtypeStruct((2, 16, 128), f32)...  78.9 us
    unnamed x2, local copies, waits for them, and re-layouts  3.19 us

profile of v1, /device:TPU:71, one launch (start us, length us, event | category | flops | bytes accessed | tf_op | source)
XLA Modules:
  0.0 83.4 jit_solution(11247669759730274950)
XLA Ops:
  1.3 78.9 %window.1 = (f32[2,16,128]{2,1,0:T(8,128)}, f32[1,2,512,128]{3,2,1,0:T(8,128)}) custom-call(f32[2,512,128]{2,1,0:T(8,128)} %kappa_ref.1, f32[1,2,512,128]{3,2,1,0:T(8,128)} %now_ref.1, f32[1,2,512,128]{3,2,1,0:T(8,128)} %before_ref.1, f32[1,4]{1,0:T(1,128)} %wavelet_ref.1, s32[1]{0:T(128)S(6)} %copy.11.source_ref, s32[1,2048]{1,0:T(1,128)} %receiver_ref.1, ...), custom_call_target="tpu_custom_call" | custom-call | tf_op jit(solution)/shard_map/window/pallas_call | solution.py:392
  80.2 1.3 %copy.12 = f32[2,16,128]{2,1,0:T(8,128)} copy(f32[2,16,128]{2,1,0:T(8,128)} %get-tuple-element.4) | data formatting | bytes 32768
  81.6 1.9 %copy.13 = f32[1,2,512,128]{3,2,1,0:T(8,128)} copy(f32[1,2,512,128]{3,2,1,0:T(8,128)} %get-tuple-element.5) | data formatting | bytes 1048576

commit v2 on v1

--- a/solution.py
+++ b/solution.py
@@ -13,7 +13,9 @@
 SHIFT = 248
 PAD = 8
 BLOCK = 24
-CHUNKS = ((0, 96), (96, 96), (192, 72))
+CHUNKS = ((0, 48), (48, 48), (96, 48), (144, 48), (192, 48), (240, 24))
+INNER = (1, 2)
+OUTER = (0, 3)
 CELL_ROWS = PLANES * ROWS
 TILE = 352
 COLUMNS = 9 * 128
@@ -23,10 +25,10 @@
 def kernel(
     kappa_ref, now_ref, before_ref, wavelet_ref, source_ref, receiver_ref, observed_ref,
     gradient_ref, next_ref,
-    u, model, source, laps, counts, adjoint, weighted, halo, image,
-    onehot_rows, onehot_lanes, kappa_rows, kappa_rim, mate, summed, landed,
+    u, model, laps, counts, adjoint, weighted, halo, image, cells, values_seen,
+    onehot_rows, onehot_lanes, kappa_rows, kappa_rim, mate, shared, crossed, gathered, landed,
     local_sem, pair_send, pair_recv, rim_send, rim_recv, halo_send, halo_recv,
-    next_sem, core_send, core_recv, band_send, band_recv,
+    next_sem, core_send, core_recv, ring_send, ring_recv, band_send, band_recv,
 ):
     shot = lax.axis_index("shot")
     dom = lax.axis_index("dom")
@@ -42,7 +44,7 @@
     last_dom = (shot, lax.rem(dom + 15, 16))
     other = (shot, lax.rem(dom + 15 + 2 * h, 16))
     twin = (shot + 1 - 2 * core, dom)
-    in_half = z // 4 == h
+    x = 2 * h + x_lo
     has_below = slab > 0
     has_above = slab < 7
 
@@ -51,14 +53,13 @@
             src_ref=src, dst_ref=dst, send_sem=send, recv_sem=recv, device_id=device, device_id_type=MESH
         )
 
-    def owner(j):
-        brick, lo, quarter = j // 8, lax.rem(j // 4, 2), lax.rem(j, 4)
-        mine = (brick == h) & (lo == x_lo) & (4 * h + quarter == z)
-        return brick, lo, quarter, mine, ((4 * h + quarter) * 4 + lo * 2 + core, 2 * slab + brick)
-
-    def giver(j):
-        mine = in_half & (j == z * 2 + x_lo)
-        return mine, (j * 2 + core, 2 * slab + z // 4)
+    def ring_device(k):
+        at = lax.rem(x + k, 4)
+        return at, (z * 4 + lax.rem(at, 2) * 2 + core, 2 * slab + at // 2)
+
+    def stack_device(k):
+        at = lax.rem(z + k, 8)
+        return at, (at * 4 + x_lo * 2 + core, dom)
 
     mine_rows = pl.ds(pl.multiple_of(h * SHIFT, 8), ROWS)
     pair_rows = pl.ds(pl.multiple_of((1 - h) * SHIFT, 8), ROWS)
@@ -66,7 +67,15 @@
     theirs = pl.ds(2 - 2 * h, 2)
     body = pl.ds(PAD, ROWS)
 
+    barrier = pltpu.get_barrier_semaphore()
+    greeted = [pair, above, below, other, twin, ring_device(1)[1], ring_device(3)[1]]
+    greeted += [stack_device(k)[1] for k in range(1, 8)]
+    for device in greeted:
+        pl.semaphore_signal(barrier, inc=1, device_id=device, device_id_type=MESH)
+
     loads = [
+        pltpu.make_async_copy(receiver_ref, cells, local_sem.at[4]),
+        pltpu.make_async_copy(observed_ref, values_seen, local_sem.at[5]),
         pltpu.make_async_copy(now_ref.at[0, :, mine_rows], u.at[1, own, body], local_sem.at[0]),
         pltpu.make_async_copy(kappa_ref.at[:, mine_rows], model.at[own], local_sem.at[1]),
         pltpu.make_async_copy(before_ref.at[0, :, mine_rows], u.at[0, own, body], local_sem.at[2]),
@@ -74,28 +83,7 @@
     ]
     for load in loads:
         load.start()
-
-    barrier = pltpu.get_barrier_semaphore()
-    for device in (pair, above, below, other, twin):
-        pl.semaphore_signal(barrier, inc=1, device_id=device, device_id_type=MESH)
-
-    def greet(j, carry):
-        _, _, _, mine, device = owner(j)
-
-        @pl.when(jnp.logical_not(mine))
-        def _():
-            pl.semaphore_signal(barrier, inc=1, device_id=device, device_id_type=MESH)
-
-        mine_too, device_too = giver(j)
-
-        @pl.when(jnp.logical_not(mine_too))
-        def _():
-            pl.semaphore_signal(barrier, inc=1, device_id=device_too, device_id_type=MESH)
-
-        return carry
-
-    lax.fori_loop(0, 16, greet, 0)
-    pl.semaphore_wait(barrier, 37 - 2 * in_half.astype(jnp.int32))
+    pl.semaphore_wait(barrier, len(greeted))
 
     exchange = [
         copy_to(pair, now_ref.at[0, :, pair_rows], u.at[1, own, body], pair_send.at[0], pair_recv.at[0]),
@@ -124,7 +112,9 @@
         kappa_rows[p, 0:PAD] = jnp.zeros((PAD, 128), jnp.float32)
         kappa_rows[p, PAD + 512 : 2 * PAD + 512] = jnp.zeros((PAD, 128), jnp.float32)
 
-    cell = receiver_ref[...]
+    loads[0].wait()
+    loads[1].wait()
+    cell = cells[...]
     plane = lax.shift_right_logical(cell, 16) - PLANES * slab
     row = lax.bitwise_and(lax.shift_right_logical(cell, 7), 511) - SHIFT * h
     inside = (plane >= 0) & (plane < PLANES) & (row >= 0) & (row < ROWS)
@@ -139,7 +129,7 @@
 
     lax.fori_loop(0, CELL_ROWS // 16, fill_rows, 0)
 
-    values = observed_ref[0]
+    values = values_seen[0]
     high = values.astype(jnp.bfloat16).astype(jnp.float32)
     low = values - high
 
@@ -211,7 +201,7 @@
                     miss = counts[0, pl.ds(p * ROWS + r, BLOCK)] * after - counts[NT, pl.ds(p * ROWS + r, BLOCK)]
                     adjoint[0, p, pl.ds(r, BLOCK)] = miss
                     weighted[0, p, pl.ds(PAD + r, BLOCK)] = speed * miss
-                    image[p, pl.ds(r, BLOCK)] = miss * lap
+                    image[int(p in OUTER), p // 2, pl.ds(r, BLOCK)] = miss * lap
             return carry
 
         lax.fori_loop(0, size // BLOCK, block, 0)
@@ -228,7 +218,7 @@
                 field = 2.0 * adjoint[j, p, pl.ds(r, BLOCK)] + lap + miss
                 if j > 0:
                     field = field - adjoint[j - 1, p, pl.ds(r, BLOCK)]
-                image[p, pl.ds(r, BLOCK)] += field * laps[level - 1, p, pl.ds(r, BLOCK)]
+                image[int(p in OUTER), p // 2, pl.ds(r, BLOCK)] += field * laps[level - 1, p, pl.ds(r, BLOCK)]
                 if level > 1:
                     adjoint[j + 1, p, pl.ds(r, BLOCK)] = field
                     weighted[j + 1, p, pl.ds(PAD + r, BLOCK)] = model[p, pl.ds(r, BLOCK)] * field
@@ -251,21 +241,21 @@
             copy.start()
             halos.append(copy)
 
-    loads[0].wait()
+    loads[2].wait()
     exchange[0].wait_recv()
     for c in range(len(CHUNKS)):
         send_rims(u.at[1], 0, c)
-    for load in loads[1:]:
+    for load in loads[3:]:
         load.wait()
     exchange[1].wait_recv()
     exchange[2].wait_recv()
 
     for n in range(NT):
-        forward(n, (1, 2), 0, ROWS)
+        forward(n, INNER, 0, ROWS)
         for c, (first, size) in enumerate(CHUNKS):
             for copy in rim_copies(u.at[n + 1], n, c):
                 copy.wait_recv()
-            forward(n, (0, 3), first, size)
+            forward(n, OUTER, first, size)
             if n < NT - 1:
                 send_rims(u.at[n + 2], n + 1, c)
             else:
@@ -278,54 +268,80 @@
     store.start()
     give.start()
 
+    def band(j, parity):
+        return pl.ds(pl.multiple_of(8 * h + 16 * (2 * j + parity), 8), 16)
+
+    def core_copy(part, j):
+        return copy_to(
+            twin, image.at[part, :, band(j, 1 - core)], mate.at[part, j], core_send.at[part, j], core_recv.at[part, j]
+        )
+
+    def core_start(part):
+        def step(j, carry):
+            core_copy(part, j).start()
+            return carry
+
+        lax.fori_loop(0, 8, step, 0)
+
+    def ring_copy(part, k):
+        at, device = ring_device(k)
+        src = shared.at[part, at // 2, lax.rem(at, 2)]
+        return copy_to(device, src, crossed.at[part, x], ring_send.at[part, k], ring_recv.at[part, x])
+
+    def core_finish(part):
+        def step(j, carry):
+            core_copy(part, j).wait_recv()
+            shared[part, :, lax.rem(j, 2), j // 2] = image[part, :, band(j, core)] + mate[part, j]
+            return carry
+
+        lax.fori_loop(0, 8, step, 0)
+        for k in range(1, 4):
+            ring_copy(part, k).start()
+        crossed[part, x] = shared[part, h, x_lo]
+
+    def stack_copy(part, k):
+        at, device = stack_device(k)
+        return copy_to(device, gathered.at[part, at], landed.at[part, z], band_send.at[part, k], band_recv.at[part, z])
+
+    def ring_finish(part):
+        for k in range(1, 4):
+            at, _ = ring_device(k)
+            copy_to(twin, crossed.at[part, at], crossed.at[part, at], ring_send.at[part, k], ring_recv.at[part, at]).wait_recv()
+
+        def step(j, carry):
+            gathered[part, j] = crossed[part, 0, j] + crossed[part, 1, j]
+            gathered[part, 4 + j] = crossed[part, 2, j] + crossed[part, 3, j]
+            return carry
+
+        lax.fori_loop(0, 4, step, 0)
+        for k in range(1, 8):
+            stack_copy(part, k).start()
+        landed[part, z] = gathered[part, z]
+
+    def stack_finish(part):
+        for k in range(1, 8):
+            at, _ = stack_device(k)
+            copy_to(twin, landed.at[part, at], landed.at[part, at], band_send.at[part, k], band_recv.at[part, at]).wait_recv()
+        total = landed[part, 0]
+        for j in range(1, 8):
+            total = total + landed[part, j]
+        plane_at = h if part else 1 - h
+        gradient_ref[plane_at] = total / NT - gradient_ref[plane_at]
+
     for j in range(NT - 1):
-        backward(j, (1, 2), 0, ROWS)
+        backward(j, INNER, 0, ROWS)
+        if j == NT - 2:
+            core_start(0)
+            core_finish(0)
         for c, (first, size) in enumerate(CHUNKS):
             for copy in rim_copies(weighted.at[j], NT + j, c):
                 copy.wait_recv()
-            backward(j, (0, 3), first, size)
+            backward(j, OUTER, first, size)
             if j < NT - 2:
                 send_rims(weighted.at[j + 1], NT + j + 1, c)
-
-    def band(j, parity):
-        return pl.ds(pl.multiple_of(8 * h + 16 * (2 * j + parity), 8), 16)
-
-    def core_copy(j):
-        return copy_to(twin, image.at[:, band(j, 1 - core)], mate.at[j], core_send.at[j], core_recv.at[j])
-
-    def core_start(j, carry):
-        core_copy(j).start()
-        return carry
-
-    def core_sum(j, carry):
-        core_copy(j).wait_recv()
-        summed[j] = image[:, band(j, core)] + mate[j]
-        return carry
-
-    lax.fori_loop(0, 8, core_start, 0)
-    lax.fori_loop(0, 8, core_sum, 0)
-
-    slot = z * 2 + x_lo
-
-    def band_copy(j):
-        brick, lo, quarter, mine, device = owner(j)
-        src = summed.at[quarter * 2 + lo, pl.ds(2 * brick, 2)]
-        return mine, copy_to(device, src, landed.at[slot], band_send.at[j], band_recv.at[slot])
-
-    def band_start(j, carry):
-        mine, copy = band_copy(j)
-
-        @pl.when(jnp.logical_not(mine))
-        def _():
-            copy.start()
-
-        return carry
-
-    lax.fori_loop(0, 16, band_start, 0)
-
-    @pl.when(in_half)
-    def _():
-        landed[slot] = summed[(z - 4 * h) * 2 + x_lo, pl.ds(2 * h, 2)]
+    core_start(1)
+    ring_finish(0)
+    core_finish(1)
 
     for copy in rims:
         copy.wait_recv()
@@ -346,40 +362,24 @@
         total = total + jnp.where(band_lanes == 0, 0.0, pltpu.roll(middle, 1, 1))
         gradient_ref[p] = (total / 6.0 - middle) * PRIOR_GAIN
 
-    def band_wait(j, carry):
-        mine, _ = giver(j)
-
-        @pl.when(jnp.logical_not(mine))
-        def _():
-            copy_to(twin, landed.at[j], landed.at[j], band_send.at[j], band_recv.at[j]).wait_recv()
-
-        return carry
-
-    lax.fori_loop(0, 16, band_wait, 0)
-    total = landed[0]
-    for j in range(1, 16):
-        total = total + landed[j]
-    gradient_ref[...] = total / NT - gradient_ref[...]
-
-    def band_done(j, carry):
-        mine, copy = band_copy(j)
-
-        @pl.when(jnp.logical_not(mine))
-        def _():
-            copy.wait_send()
-
-        return carry
-
-    def core_done(j, carry):
-        core_copy(j).wait_send()
-        return carry
-
+    ring_finish(1)
+    stack_finish(0)
+    stack_finish(1)
+
+    for part in range(2):
+        def step(j, carry):
+            core_copy(part, j).wait_send()
+            return carry
+
+        lax.fori_loop(0, 8, step, 0)
+        for k in range(1, 4):
+            ring_copy(part, k).wait_send()
+        for k in range(1, 8):
+            stack_copy(part, k).wait_send()
     store.wait()
     give.wait()
     for copy in exchange + rims + halos:
         copy.wait_send()
-    lax.fori_loop(0, 8, core_done, 0)
-    lax.fori_loop(0, 16, band_done, 0)
 
 
 def shards(kappa, wave_now, wave_before, wavelet, source_cell, receiver_cells, observed):
@@ -395,26 +395,29 @@
             jax.ShapeDtypeStruct((2, 16, 128), f32),
             jax.ShapeDtypeStruct(wave_now.shape, f32),
         ),
-        in_specs=[anywhere, anywhere, anywhere, smem, smem, vmem, vmem],
+        in_specs=[anywhere, anywhere, anywhere, smem, smem, anywhere, anywhere],
         out_specs=(vmem, anywhere),
         scratch_shapes=[
             pltpu.VMEM((6, PLANES, ROWS + 2 * PAD, 128), f32),
             pltpu.VMEM((PLANES, ROWS, 128), f32),
-            pltpu.VMEM((8, 128), f32),
             pltpu.VMEM((3, PLANES, ROWS, 128), f32),
             pltpu.VMEM((5, CELL_ROWS, 128), f32),
             pltpu.VMEM((3, PLANES, ROWS, 128), f32),
             pltpu.VMEM((3, PLANES, ROWS + 2 * PAD, 128), f32),
             pltpu.VMEM((7, 2, ROWS, 128), f32),
-            pltpu.VMEM((PLANES, ROWS, 128), f32),
+            pltpu.VMEM((2, 2, ROWS, 128), f32),
+            pltpu.VMEM((1, 2048), jnp.int32),
+            pltpu.VMEM((1, NT, 2048), f32),
             pltpu.VMEM((CELL_ROWS, 2048), jnp.bfloat16),
             pltpu.VMEM((COLUMNS, 2048), jnp.bfloat16),
             pltpu.VMEM((2, 512 + 2 * PAD, 128), f32),
             pltpu.VMEM((2, 16, 128), f32),
-            pltpu.VMEM((8, PLANES, 16, 128), f32),
-            pltpu.VMEM((8, PLANES, 16, 128), f32),
-            pltpu.VMEM((16, 2, 16, 128), f32),
-            dma((4,)),
+            pltpu.VMEM((2, 8, 2, 16, 128), f32),
+            pltpu.VMEM((2, 2, 2, 4, 16, 128), f32),
+            pltpu.VMEM((2, 4, 4, 16, 128), f32),
+            pltpu.VMEM((2, 8, 16, 128), f32),
+            pltpu.VMEM((2, 8, 16, 128), f32),
+            dma((6,)),
             dma((3,)),
             dma((3,)),
             dma((2,)),
@@ -422,10 +425,12 @@
             dma((7, chunks, 2)),
             dma((7, chunks, 2)),
             dma((3,)),
-            dma((8,)),
-            dma((8,)),
-            dma((16,)),
-            dma((16,)),
+            dma((2, 8)),
+            dma((2, 8)),
+            dma((2, 4)),
+            dma((2, 4)),
+            dma((2, 8)),
+            dma((2, 8)),
         ],
         name="window",
         compiler_params=pltpu.CompilerParams(

time: 83.7 us -> 78.7 us (0.940)
  the two profiles are of different devices: /device:TPU:71 before, /device:TPU:1 now
where the time goes in v2:
time: 78.7 us; the launch traced here: 78.5 us
  Pallas kernels  74 us (94%)
  local copies, waits for them, and re-layouts  3.19 us (4%)
  between operations  1.29 us (2%)
    pallas_call x1, Pallas kernels, shards(): pl.pallas_call(kernel, out_shape=(jax.ShapeDtypeStruct((2, 16, 128), f32)...  74 us
    unnamed x2, local copies, waits for them, and re-layouts  3.19 us

profile of v2, /device:TPU:1, one launch (start us, length us, event | category | flops | bytes accessed | tf_op | source)
XLA Modules:
  0.0 78.5 jit_solution(6807552422654694934)
XLA Ops:
  1.3 74.0 %window.1 = (f32[2,16,128]{2,1,0:T(8,128)}, f32[1,2,512,128]{3,2,1,0:T(8,128)}) custom-call(f32[2,512,128]{2,1,0:T(8,128)} %kappa_ref.1, f32[1,2,512,128]{3,2,1,0:T(8,128)} %now_ref.1, f32[1,2,512,128]{3,2,1,0:T(8,128)} %before_ref.1, f32[1,4]{1,0:T(1,128)} %wavelet_ref.1, s32[1]{0:T(128)S(6)} %copy.11.source_ref, s32[1,2048]{1,0:T(1,128)} %receiver_ref.1, ...), custom_call_target="tpu_custom_call" | custom-call | tf_op jit(solution)/shard_map/window/pallas_call | solution.py:392
  75.3 1.3 %copy.12 = f32[2,16,128]{2,1,0:T(8,128)} copy(f32[2,16,128]{2,1,0:T(8,128)} %get-tuple-element.4) | data formatting | bytes 32768
  76.6 1.9 %copy.13 = f32[1,2,512,128]{3,2,1,0:T(8,128)} copy(f32[1,2,512,128]{3,2,1,0:T(8,128)} %get-tuple-element.5) | data formatting | bytes 1048576

commit v3 on v2

--- a/solution.py
+++ b/solution.py
@@ -19,6 +19,7 @@
 CELL_ROWS = PLANES * ROWS
 TILE = 352
 COLUMNS = 9 * 128
+PIECES = 2
 MESH = pl.DeviceIdType.MESH
 
 
@@ -27,7 +28,7 @@
     gradient_ref, next_ref,
     u, model, laps, counts, adjoint, weighted, halo, image, cells, values_seen,
     onehot_rows, onehot_lanes, kappa_rows, kappa_rim, mate, shared, crossed, gathered, landed,
-    local_sem, pair_send, pair_recv, rim_send, rim_recv, halo_send, halo_recv,
+    local_sem, pair_send, pair_recv, share_send, share_recv, rim_send, rim_recv, halo_send, halo_recv,
     next_sem, core_send, core_recv, ring_send, ring_recv, band_send, band_recv,
 ):
     shot = lax.axis_index("shot")
@@ -85,9 +86,18 @@
         load.start()
     pl.semaphore_wait(barrier, len(greeted))
 
+    def share(first, size):
+        return pl.ds(pl.multiple_of(first, 8), size)
+
+    eighth = share(z * 32, 32)
     exchange = [
+        copy_to(
+            pair, kappa_ref.at[:, share((1 - h) * SHIFT + z * 32, 32)], model.at[own, eighth], pair_send.at[1], pair_recv.at[1]
+        ),
+        copy_to(
+            pair, kappa_ref.at[:, share((1 - h) * SHIFT + 256, 8)], model.at[own, 256:264], pair_send.at[3], pair_recv.at[3]
+        ),
         copy_to(pair, now_ref.at[0, :, pair_rows], u.at[1, own, body], pair_send.at[0], pair_recv.at[0]),
-        copy_to(pair, kappa_ref.at[:, pair_rows], model.at[own], pair_send.at[1], pair_recv.at[1]),
         copy_to(pair, before_ref.at[0, :, pair_rows], u.at[0, own, body], pair_send.at[2], pair_recv.at[2]),
     ]
     for copy in exchange:
@@ -128,6 +138,14 @@
         return carry
 
     lax.fori_loop(0, CELL_ROWS // 16, fill_rows, 0)
+
+    exchange[0].wait_recv()
+    passed = []
+    for k in range(1, 8):
+        part = model.at[theirs, eighth]
+        passed.append(copy_to(stack_device(k)[1], part, part, share_send.at[k], share_recv.at[z]))
+    for copy in passed:
+        copy.start()
 
     values = values_seen[0]
     high = values.astype(jnp.bfloat16).astype(jnp.float32)
@@ -242,13 +260,17 @@
             halos.append(copy)
 
     loads[2].wait()
-    exchange[0].wait_recv()
+    exchange[2].wait_recv()
     for c in range(len(CHUNKS)):
         send_rims(u.at[1], 0, c)
     for load in loads[3:]:
         load.wait()
     exchange[1].wait_recv()
-    exchange[2].wait_recv()
+    for k in range(1, 8):
+        at, device = stack_device(k)
+        part = model.at[theirs, share(at * 32, 32)]
+        copy_to(device, part, part, share_send.at[k], share_recv.at[at]).wait_recv()
+    exchange[3].wait_recv()
 
     for n in range(NT):
         forward(n, INNER, 0, ROWS)
@@ -378,8 +400,27 @@
             stack_copy(part, k).wait_send()
     store.wait()
     give.wait()
-    for copy in exchange + rims + halos:
+    for copy in exchange + passed + rims + halos:
         copy.wait_send()
+
+
+def hand_over(gradient_ref, next_ref, gradient_out, next_out, gradient, waves, load_sem, store_sem):
+    loads, stores = [], []
+    for p in range(2):
+        for i in range(PIECES):
+            rows = pl.ds(i * (512 // PIECES), 512 // PIECES)
+            at = 1 + p * PIECES + i
+            loads.append(pltpu.make_async_copy(next_ref.at[0, p, rows], waves.at[p, rows], load_sem.at[at]))
+            stores.append(pltpu.make_async_copy(waves.at[p, rows], next_out.at[0, p, rows], store_sem.at[at]))
+    loads.append(pltpu.make_async_copy(gradient_ref, gradient, load_sem.at[0]))
+    stores.append(pltpu.make_async_copy(gradient, gradient_out, store_sem.at[0]))
+    for load in loads:
+        load.start()
+    for load, store in zip(loads, stores):
+        load.wait()
+        store.start()
+    for store in stores:
+        store.wait()
 
 
 def shards(kappa, wave_now, wave_before, wavelet, source_cell, receiver_cells, observed):
@@ -389,7 +430,7 @@
     vmem = pl.BlockSpec(memory_space=pltpu.VMEM)
     smem = pl.BlockSpec(memory_space=pltpu.SMEM)
     dma = pltpu.SemaphoreType.DMA
-    return pl.pallas_call(
+    results = pl.pallas_call(
         kernel,
         out_shape=(
             jax.ShapeDtypeStruct((2, 16, 128), f32),
@@ -418,8 +459,10 @@
             pltpu.VMEM((2, 8, 16, 128), f32),
             pltpu.VMEM((2, 8, 16, 128), f32),
             dma((6,)),
-            dma((3,)),
-            dma((3,)),
+            dma((4,)),
+            dma((4,)),
+            dma((8,)),
+            dma((8,)),
             dma((2,)),
             dma((2,)),
             dma((7, chunks, 2)),
@@ -437,6 +480,19 @@
             collective_id=0, has_side_effects=True, vmem_limit_bytes=56 << 20
         ),
     )(kappa, wave_now, wave_before, wavelet, source_cell, receiver_cells, observed)
+    return pl.pallas_call(
+        hand_over,
+        out_shape=tuple(jax.ShapeDtypeStruct(r.shape, r.dtype) for r in results),
+        in_specs=[anywhere, anywhere],
+        out_specs=(anywhere, anywhere),
+        scratch_shapes=[
+            pltpu.VMEM((2, 16, 128), f32),
+            pltpu.VMEM((2, 512, 128), f32),
+            dma((1 + 2 * PIECES,)),
+            dma((1 + 2 * PIECES,)),
+        ],
+        name="hand_over",
+    )(*results)
 
 
 def solution(mesh):

time: 78.7 us -> 72.5 us (0.921)
  local copies, waits for them, and re-layouts: 3.19 us -> 0 us
  Pallas kernels: 74 us -> 71.1 us
    pallas_call x1, Pallas kernels: 74 us -> 69.3 us  [shards(): pl.pallas_call(kernel, out_shape=(jax.ShapeDtypeStruct((2, 16, 128), f32)...]
    unnamed x2 -> x0, local copies, waits for them, and re-layouts: 3.19 us -> none
    pallas_call x0 -> x1, Pallas kernels: none -> 1.84 us  [shards(): pl.pallas_call(hand_over, out_shape=tuple((jax.ShapeDtypeStruct(r.shape,...]
where the time goes in v3:
time: 72.5 us; the launch traced here: 72.4 us
  Pallas kernels  71.1 us (98%)
  between operations  1.29 us (2%)
    pallas_call x1, Pallas kernels, shards(): pl.pallas_call(kernel, out_shape=(jax.ShapeDtypeStruct((2, 16, 128), f32)...  69.3 us
    pallas_call x1, Pallas kernels, shards(): pl.pallas_call(hand_over, out_shape=tuple((jax.ShapeDtypeStruct(r.shape,...  1.84 us

profile of v3, /device:TPU:1, one launch (start us, length us, event | category | flops | bytes accessed | tf_op | source)
XLA Modules:
  0.0 72.4 jit_solution(8807375953152329607)
XLA Ops:
  1.3 69.3 %window.1 = (f32[2,16,128]{2,1,0:T(8,128)}, f32[1,2,512,128]{3,2,1,0:T(8,128)}) custom-call(f32[2,512,128]{2,1,0:T(8,128)} %kappa_ref.1, f32[1,2,512,128]{3,2,1,0:T(8,128)} %now_ref.1, f32[1,2,512,128]{3,2,1,0:T(8,128)} %before_ref.1, f32[1,4]{1,0:T(1,128)} %wavelet_ref.1, s32[1]{0:T(128)S(6)} %copy.9.source_ref, s32[1,2048]{1,0:T(1,128)} %receiver_ref.1, ...), custom_call_target="tpu_custom_call" | custom-call | tf_op jit(solution)/shard_map/window/pallas_call | solution.py:433
  70.5 1.8 %hand_over.1 = (f32[2,16,128]{2,1,0:T(8,128)}, f32[1,2,512,128]{3,2,1,0:T(8,128)}) custom-call(f32[2,16,128]{2,1,0:T(8,128)} %get-tuple-element.4.gradient_ref, f32[1,2,512,128]{3,2,1,0:T(8,128)} %get-tuple-element.5.next_ref), custom_call_target="tpu_custom_call" | custom-call | tf_op jit(solution)/shard_map/hand_over/pallas_call | solution.py:483

commit v4 on v3

--- a/solution.py
+++ b/solution.py
@@ -14,6 +14,8 @@
 PAD = 8
 BLOCK = 24
 CHUNKS = ((0, 48), (48, 48), (96, 48), (144, 48), (192, 48), (240, 24))
+HALVES = ((0, 144), (144, 120))
+LATER = (2, 2, 3, 3)
 INNER = (1, 2)
 OUTER = (0, 3)
 CELL_ROWS = PLANES * ROWS
@@ -28,7 +30,7 @@
     gradient_ref, next_ref,
     u, model, laps, counts, adjoint, weighted, halo, image, cells, values_seen,
     onehot_rows, onehot_lanes, kappa_rows, kappa_rim, mate, shared, crossed, gathered, landed,
-    local_sem, pair_send, pair_recv, share_send, share_recv, rim_send, rim_recv, halo_send, halo_recv,
+    local_sem, pair_send, pair_recv, share_send, share_recv, first_send, first_recv, rim_send, rim_recv, halo_send, halo_recv,
     next_sem, core_send, core_recv, ring_send, ring_recv, band_send, band_recv,
 ):
     shot = lax.axis_index("shot")
@@ -84,32 +86,6 @@
     ]
     for load in loads:
         load.start()
-    pl.semaphore_wait(barrier, len(greeted))
-
-    def share(first, size):
-        return pl.ds(pl.multiple_of(first, 8), size)
-
-    eighth = share(z * 32, 32)
-    exchange = [
-        copy_to(
-            pair, kappa_ref.at[:, share((1 - h) * SHIFT + z * 32, 32)], model.at[own, eighth], pair_send.at[1], pair_recv.at[1]
-        ),
-        copy_to(
-            pair, kappa_ref.at[:, share((1 - h) * SHIFT + 256, 8)], model.at[own, 256:264], pair_send.at[3], pair_recv.at[3]
-        ),
-        copy_to(pair, now_ref.at[0, :, pair_rows], u.at[1, own, body], pair_send.at[0], pair_recv.at[0]),
-        copy_to(pair, before_ref.at[0, :, pair_rows], u.at[0, own, body], pair_send.at[2], pair_recv.at[2]),
-    ]
-    for copy in exchange:
-        copy.start()
-    band_rows = pl.ds(pl.multiple_of(shot * 16, 8), 16)
-    rims = [
-        copy_to(next_dom, kappa_ref.at[1, band_rows], kappa_rim.at[0], rim_send.at[0], rim_recv.at[0]),
-        copy_to(last_dom, kappa_ref.at[0, band_rows], kappa_rim.at[1], rim_send.at[1], rim_recv.at[1]),
-    ]
-    for copy in rims:
-        copy.start()
-
     for n in range(6):
         for p in range(PLANES):
             u[n, p, 0:PAD] = jnp.zeros((PAD, 128), jnp.float32)
@@ -123,7 +99,6 @@
         kappa_rows[p, PAD + 512 : 2 * PAD + 512] = jnp.zeros((PAD, 128), jnp.float32)
 
     loads[0].wait()
-    loads[1].wait()
     cell = cells[...]
     plane = lax.shift_right_logical(cell, 16) - PLANES * slab
     row = lax.bitwise_and(lax.shift_right_logical(cell, 7), 511) - SHIFT * h
@@ -138,15 +113,79 @@
         return carry
 
     lax.fori_loop(0, CELL_ROWS // 16, fill_rows, 0)
+    pl.semaphore_wait(barrier, len(greeted))
+
+    def share(first, size):
+        return pl.ds(pl.multiple_of(first, 8), size)
+
+    eighth = share(z * 32, 32)
+
+    def outer_copy(i):
+        first, size = HALVES[i]
+        src = now_ref.at[0, h, share((1 - h) * SHIFT + first, size)]
+        return copy_to(pair, src, u.at[1, 3 * h, pl.ds(PAD + first, size)], pair_send.at[4 + i], pair_recv.at[4 + i])
+
+    def relay(i):
+        first, size = HALVES[i]
+        device = (shot, lax.rem(dom + 2 + 12 * h, 16))
+        src = u.at[1, 3 - 3 * h, pl.ds(PAD + first, size)]
+        return copy_to(device, src, halo.at[0, h, pl.ds(first, size)], first_send.at[i], first_recv.at[i])
+
+    direct = copy_to(
+        (shot, lax.rem(dom + 14 + 4 * h, 16)), now_ref.at[0, h, mine_rows], halo.at[0, 1 - h], first_send.at[2], first_recv.at[2]
+    )
+    opening = [relay(0), relay(1), direct]
+
+    def kappa_copy(i):
+        src = kappa_ref.at[(h, 1 - h)[i], share((1 - h) * SHIFT + z * 32, 32)]
+        return copy_to(pair, src, model.at[(3 * h, 1 + h)[i], eighth], pair_send.at[i], pair_recv.at[i])
+
+    def before_copy(i):
+        src = before_ref.at[0, (h, 1 - h)[i], pair_rows]
+        return copy_to(pair, src, u.at[0, (3 * h, 1 + h)[i], body], pair_send.at[6 + i], pair_recv.at[6 + i])
+
+    exchange = [
+        kappa_copy(0),
+        copy_to(
+            pair, kappa_ref.at[:, share((1 - h) * SHIFT + 256, 8)], model.at[own, 256:264], pair_send.at[2], pair_recv.at[2]
+        ),
+        outer_copy(0),
+        outer_copy(1),
+        copy_to(pair, now_ref.at[0, 1 - h, pair_rows], u.at[1, 1 + h, body], pair_send.at[3], pair_recv.at[3]),
+        kappa_copy(1),
+        before_copy(0),
+        before_copy(1),
+    ]
+    direct.start()
+    for copy in exchange:
+        copy.start()
+    band_rows = pl.ds(pl.multiple_of(shot * 16, 8), 16)
+    rims = [
+        copy_to(next_dom, kappa_ref.at[1, band_rows], kappa_rim.at[0], rim_send.at[0], rim_recv.at[0]),
+        copy_to(last_dom, kappa_ref.at[0, band_rows], kappa_rim.at[1], rim_send.at[1], rim_recv.at[1]),
+    ]
+    for copy in rims:
+        copy.start()
+
+    passed = []
+
+    def pass_on(i):
+        part = model.at[(3 - 3 * h, 2 - h)[i], eighth]
+        for k in range(1, 8):
+            copy = copy_to(stack_device(k)[1], part, part, share_send.at[i, k], share_recv.at[i, z])
+            copy.start()
+            passed.append(copy)
+
+    def take_over(i):
+        for k in range(1, 8):
+            at, device = stack_device(k)
+            part = model.at[(3 - 3 * h, 2 - h)[i], share(at * 32, 32)]
+            copy_to(device, part, part, share_send.at[i, k], share_recv.at[i, at]).wait_recv()
 
     exchange[0].wait_recv()
-    passed = []
-    for k in range(1, 8):
-        part = model.at[theirs, eighth]
-        passed.append(copy_to(stack_device(k)[1], part, part, share_send.at[k], share_recv.at[z]))
-    for copy in passed:
-        copy.start()
-
+    pass_on(0)
+
+    loads[1].wait()
     values = values_seen[0]
     high = values.astype(jnp.bfloat16).astype(jnp.float32)
     low = values - high
@@ -175,7 +214,12 @@
             )
         return carry
 
-    lax.fori_loop(0, CELL_ROWS // TILE, spread, 0)
+    for i in range(2):
+        exchange[2 + i].wait_recv()
+        opening[i].start()
+    lax.fori_loop(0, LATER[0], spread, 0)
+    exchange[5].wait_recv()
+    pass_on(1)
 
     spot = source_ref[0]
     spot_plane = lax.shift_right_logical(spot, 16) - PLANES * slab
@@ -259,29 +303,32 @@
             copy.start()
             halos.append(copy)
 
-    loads[2].wait()
-    exchange[2].wait_recv()
-    for c in range(len(CHUNKS)):
-        send_rims(u.at[1], 0, c)
-    for load in loads[3:]:
+    for load in loads[2:]:
         load.wait()
-    exchange[1].wait_recv()
-    for k in range(1, 8):
-        at, device = stack_device(k)
-        part = model.at[theirs, share(at * 32, 32)]
-        copy_to(device, part, part, share_send.at[k], share_recv.at[at]).wait_recv()
-    exchange[3].wait_recv()
+    for i in (4, 1, 6):
+        exchange[i].wait_recv()
+    take_over(0)
+    for copy in opening:
+        copy.wait_recv()
 
     for n in range(NT):
-        forward(n, INNER, 0, ROWS)
+        if n > 0:
+            forward(n, INNER, 0, ROWS)
         for c, (first, size) in enumerate(CHUNKS):
-            for copy in rim_copies(u.at[n + 1], n, c):
-                copy.wait_recv()
+            if n > 0:
+                for copy in rim_copies(u.at[n + 1], n, c):
+                    copy.wait_recv()
             forward(n, OUTER, first, size)
             if n < NT - 1:
                 send_rims(u.at[n + 2], n + 1, c)
             else:
                 send_rims(weighted.at[0], NT, c)
+        if n == 0:
+            exchange[7].wait_recv()
+            take_over(1)
+            forward(0, INNER, 0, ROWS)
+        if n < NT - 1:
+            lax.fori_loop(LATER[n], LATER[n + 1], spread, 0)
 
     half = pl.ds(pl.multiple_of(h * 256, 8), 256)
     kept = pl.ds(pl.multiple_of(PAD + 8 * h, 8), 256)
@@ -384,11 +431,7 @@
         total = total + jnp.where(band_lanes == 0, 0.0, pltpu.roll(middle, 1, 1))
         gradient_ref[p] = (total / 6.0 - middle) * PRIOR_GAIN
 
-    ring_finish(1)
-    stack_finish(0)
-    stack_finish(1)
-
-    for part in range(2):
+    def sent(part):
         def step(j, carry):
             core_copy(part, j).wait_send()
             return carry
@@ -396,12 +439,21 @@
         lax.fori_loop(0, 8, step, 0)
         for k in range(1, 4):
             ring_copy(part, k).wait_send()
-        for k in range(1, 8):
-            stack_copy(part, k).wait_send()
+
+    for copy in exchange + passed + opening + rims + halos:
+        copy.wait_send()
     store.wait()
     give.wait()
-    for copy in exchange + passed + rims + halos:
-        copy.wait_send()
+    sent(0)
+
+    ring_finish(1)
+    stack_finish(0)
+    sent(1)
+    for k in range(1, 8):
+        stack_copy(0, k).wait_send()
+    stack_finish(1)
+    for k in range(1, 8):
+        stack_copy(1, k).wait_send()
 
 
 def hand_over(gradient_ref, next_ref, gradient_out, next_out, gradient, waves, load_sem, store_sem):
@@ -459,10 +511,12 @@
             pltpu.VMEM((2, 8, 16, 128), f32),
             pltpu.VMEM((2, 8, 16, 128), f32),
             dma((6,)),
-            dma((4,)),
-            dma((4,)),
             dma((8,)),
             dma((8,)),
+            dma((2, 8)),
+            dma((2, 8)),
+            dma((3,)),
+            dma((3,)),
             dma((2,)),
             dma((2,)),
             dma((7, chunks, 2)),

time: 72.5 us -> 71.2 us (0.982)
  Pallas kernels: 71.1 us -> 69.7 us
    pallas_call x1, Pallas kernels: 69.3 us -> 67.9 us  [shards(): pl.pallas_call(kernel, out_shape=(jax.ShapeDtypeStruct((2, 16, 128), f32)...]
where the time goes in v4:
time: 71.2 us; the launch traced here: 71 us
  Pallas kernels  69.7 us (98%)
  between operations  1.29 us (2%)
    pallas_call x1, Pallas kernels, shards(): pl.pallas_call(kernel, out_shape=(jax.ShapeDtypeStruct((2, 16, 128), f32)...  67.9 us
    pallas_call x1, Pallas kernels, shards(): pl.pallas_call(hand_over, out_shape=tuple((jax.ShapeDtypeStruct(r.shape,...  1.84 us

profile of v4, /device:TPU:1, one launch (start us, length us, event | category | flops | bytes accessed | tf_op | source)
XLA Modules:
  0.0 71.0 jit_solution(13387709252762054521)
XLA Ops:
  1.3 67.9 %window.1 = (f32[2,16,128]{2,1,0:T(8,128)}, f32[1,2,512,128]{3,2,1,0:T(8,128)}) custom-call(f32[2,512,128]{2,1,0:T(8,128)} %kappa_ref.1, f32[1,2,512,128]{3,2,1,0:T(8,128)} %now_ref.1, f32[1,2,512,128]{3,2,1,0:T(8,128)} %before_ref.1, f32[1,4]{1,0:T(1,128)} %wavelet_ref.1, s32[1]{0:T(128)S(6)} %copy.9.source_ref, s32[1,2048]{1,0:T(1,128)} %receiver_ref.1, ...), custom_call_target="tpu_custom_call" | custom-call | tf_op jit(solution)/shard_map/window/pallas_call | solution.py:485
  69.1 1.8 %hand_over.1 = (f32[2,16,128]{2,1,0:T(8,128)}, f32[1,2,512,128]{3,2,1,0:T(8,128)}) custom-call(f32[2,16,128]{2,1,0:T(8,128)} %get-tuple-element.4.gradient_ref, f32[1,2,512,128]{3,2,1,0:T(8,128)} %get-tuple-element.5.next_ref), custom_call_target="tpu_custom_call" | custom-call | tf_op jit(solution)/shard_map/hand_over/pallas_call | solution.py:537

commit v5 on v4

--- a/solution.py
+++ b/solution.py
@@ -15,7 +15,8 @@
 BLOCK = 24
 CHUNKS = ((0, 48), (48, 48), (96, 48), (144, 48), (192, 48), (240, 24))
 HALVES = ((0, 144), (144, 120))
-LATER = (2, 2, 3, 3)
+LAGGED = ((0, 24), (24, 48), (72, 48), (120, 48), (168, 48), (216, 48))
+EARLY = 2
 INNER = (1, 2)
 OUTER = (0, 3)
 CELL_ROWS = PLANES * ROWS
@@ -28,9 +29,9 @@
 def kernel(
     kappa_ref, now_ref, before_ref, wavelet_ref, source_ref, receiver_ref, observed_ref,
     gradient_ref, next_ref,
-    u, model, laps, counts, adjoint, weighted, halo, image, cells, values_seen,
+    u, model, laps, counts, adjoint, weighted, halo, near, far, model_rim, image, cells, values_seen,
     onehot_rows, onehot_lanes, kappa_rows, kappa_rim, mate, shared, crossed, gathered, landed,
-    local_sem, pair_send, pair_recv, share_send, share_recv, first_send, first_recv, rim_send, rim_recv, halo_send, halo_recv,
+    local_sem, pair_send, pair_recv, share_send, share_recv, first_send, first_recv, lean_send, lean_recv, far_send, far_recv, rim_send, rim_recv, halo_send, halo_recv,
     next_sem, core_send, core_recv, ring_send, ring_recv, band_send, band_recv,
 ):
     shot = lax.axis_index("shot")
@@ -95,6 +96,8 @@
             weighted[n, p, 0:PAD] = jnp.zeros((PAD, 128), jnp.float32)
             weighted[n, p, PAD + ROWS : 2 * PAD + ROWS] = jnp.zeros((PAD, 128), jnp.float32)
     for p in range(2):
+        near[p, 0:PAD] = jnp.zeros((PAD, 128), jnp.float32)
+        near[p, PAD + ROWS : 2 * PAD + ROWS] = jnp.zeros((PAD, 128), jnp.float32)
         kappa_rows[p, 0:PAD] = jnp.zeros((PAD, 128), jnp.float32)
         kappa_rows[p, PAD + 512 : 2 * PAD + 512] = jnp.zeros((PAD, 128), jnp.float32)
 
@@ -135,6 +138,12 @@
         (shot, lax.rem(dom + 14 + 4 * h, 16)), now_ref.at[0, h, mine_rows], halo.at[0, 1 - h], first_send.at[2], first_recv.at[2]
     )
     opening = [relay(0), relay(1), direct]
+    lean = [
+        copy_to(
+            (shot, lax.rem(dom + 14 + 4 * h, 16)), kappa_ref.at[h, mine_rows], model_rim.at[1 - h], lean_send.at[0], lean_recv.at[0]
+        ),
+        copy_to((shot, lax.rem(dom + 2 + 12 * h, 16)), model.at[3 - 3 * h], model_rim.at[h], lean_send.at[1], lean_recv.at[1]),
+    ]
 
     def kappa_copy(i):
         src = kappa_ref.at[(h, 1 - h)[i], share((1 - h) * SHIFT + z * 32, 32)]
@@ -157,6 +166,7 @@
         before_copy(1),
     ]
     direct.start()
+    lean[0].start()
     for copy in exchange:
         copy.start()
     band_rows = pl.ds(pl.multiple_of(shot * 16, 8), 16)
@@ -217,7 +227,7 @@
     for i in range(2):
         exchange[2 + i].wait_recv()
         opening[i].start()
-    lax.fori_loop(0, LATER[0], spread, 0)
+    lax.fori_loop(0, EARLY, spread, 0)
     exchange[5].wait_recv()
     pass_on(1)
 
@@ -235,22 +245,46 @@
         if p < PLANES - 1:
             after = field[p + 1, pl.ds(PAD + r, BLOCK)]
         else:
-            after = jnp.where(has_above, rim[1, pl.ds(r, BLOCK)], 0.0)
+            after = jnp.where(has_above, rim[1][pl.ds(r, BLOCK)], 0.0)
         if p > 0:
             prior = field[p - 1, pl.ds(PAD + r, BLOCK)]
         else:
-            prior = jnp.where(has_below, rim[0, pl.ds(r, BLOCK)], 0.0)
+            prior = jnp.where(has_below, rim[0][pl.ds(r, BLOCK)], 0.0)
         total = after + prior
         total = total + field[p, pl.ds(PAD + 1 + r, BLOCK)] + field[p, pl.ds(PAD - 1 + r, BLOCK)]
         total = total + jnp.where(last_lane, 0.0, pltpu.roll(middle, 127, 1))
         total = total + jnp.where(first_lane, 0.0, pltpu.roll(middle, 1, 1))
         return total - 6.0 * middle, middle
 
+    def rims_of(n):
+        if n == 2:
+            return near.at[0, pl.ds(PAD, ROWS)], near.at[1, pl.ds(PAD, ROWS)]
+        return halo.at[n, 0], halo.at[n, 1]
+
+    def edge(first, size):
+        def block(i, carry):
+            r = pl.multiple_of(first + i * BLOCK, 8)
+            for side in range(2):
+                middle = near[side, pl.ds(PAD + r, BLOCK)]
+                total = far[side, pl.ds(r, BLOCK)] + u[3, 3 * side, pl.ds(PAD + r, BLOCK)]
+                total = total + near[side, pl.ds(PAD + 1 + r, BLOCK)] + near[side, pl.ds(PAD - 1 + r, BLOCK)]
+                total = total + jnp.where(last_lane, 0.0, pltpu.roll(middle, 127, 1))
+                total = total + jnp.where(first_lane, 0.0, pltpu.roll(middle, 1, 1))
+                lap = total - 6.0 * middle
+                hit = (spot_plane == 5 * side - 1) & (spot_lane == lanes) & (spot_row - r == block_rows)
+                pulse = jnp.where(hit, wavelet_ref[0, 2], 0.0)
+                halo[3, side, pl.ds(r, BLOCK)] = (
+                    2.0 * middle - halo[1, side, pl.ds(r, BLOCK)] + model_rim[side, pl.ds(r, BLOCK)] * lap + pulse
+                )
+            return carry
+
+        lax.fori_loop(0, size // BLOCK, block, 0)
+
     def forward(n, planes, first, size):
         def block(i, carry):
             r = pl.multiple_of(first + i * BLOCK, 8)
             for p in planes:
-                lap, middle = laplace(u.at[n + 1], halo.at[n], p, r)
+                lap, middle = laplace(u.at[n + 1], rims_of(n), p, r)
                 speed = model[p, pl.ds(r, BLOCK)]
                 pulse = jnp.where(
                     (spot_plane == p) & (spot_lane == lanes) & (spot_row - r == block_rows), wavelet_ref[0, n], 0.0
@@ -274,7 +308,7 @@
         def block(i, carry):
             r = pl.multiple_of(first + i * BLOCK, 8)
             for p in planes:
-                lap, _ = laplace(weighted.at[j], halo.at[NT + j], p, r)
+                lap, _ = laplace(weighted.at[j], rims_of(NT + j), p, r)
                 at = pl.ds(p * ROWS + r, BLOCK)
                 miss = counts[0, at] * u[level + 1, p, pl.ds(PAD + r, BLOCK)] - counts[level, at]
                 field = 2.0 * adjoint[j, p, pl.ds(r, BLOCK)] + lap + miss
@@ -289,11 +323,20 @@
         lax.fori_loop(0, size // BLOCK, block, 0)
 
     def rim_copies(field, n, c):
-        first, size = CHUNKS[c]
+        first, size = LAGGED[c] if n >= NT else CHUNKS[c]
+        at, to = pl.ds(PAD + first, size), pl.ds(first, size)
+        into = (near.at[0, at], near.at[1, at]) if n == 2 else (halo.at[n, 0, to], halo.at[n, 1, to])
+        return (
+            copy_to(above, field.at[PLANES - 1, at], into[0], halo_send.at[n, c, 0], halo_recv.at[n, c, 0]),
+            copy_to(below, field.at[0, at], into[1], halo_send.at[n, c, 1], halo_recv.at[n, c, 1]),
+        )
+
+    def far_copies(i):
+        first, size = HALVES[i]
         at, to = pl.ds(PAD + first, size), pl.ds(first, size)
         return (
-            copy_to(above, field.at[PLANES - 1, at], halo.at[n, 0, to], halo_send.at[n, c, 0], halo_recv.at[n, c, 0]),
-            copy_to(below, field.at[0, at], halo.at[n, 1, to], halo_send.at[n, c, 1], halo_recv.at[n, c, 1]),
+            copy_to(above, u.at[3, 2, at], far.at[0, to], far_send.at[i, 0], far_recv.at[i, 0]),
+            copy_to(below, u.at[3, 1, at], far.at[1, to], far_send.at[i, 1], far_recv.at[i, 1]),
         )
 
     halos = []
@@ -311,24 +354,40 @@
     for copy in opening:
         copy.wait_recv()
 
-    for n in range(NT):
-        if n > 0:
-            forward(n, INNER, 0, ROWS)
-        for c, (first, size) in enumerate(CHUNKS):
-            if n > 0:
-                for copy in rim_copies(u.at[n + 1], n, c):
-                    copy.wait_recv()
-            forward(n, OUTER, first, size)
-            if n < NT - 1:
-                send_rims(u.at[n + 2], n + 1, c)
-            else:
-                send_rims(weighted.at[0], NT, c)
-        if n == 0:
-            exchange[7].wait_recv()
-            take_over(1)
-            forward(0, INNER, 0, ROWS)
-        if n < NT - 1:
-            lax.fori_loop(LATER[n], LATER[n + 1], spread, 0)
+    for c, (first, size) in enumerate(CHUNKS):
+        forward(0, OUTER, first, size)
+        send_rims(u.at[2], 1, c)
+    lean[1].start()
+    exchange[7].wait_recv()
+    take_over(1)
+    forward(0, INNER, 0, ROWS)
+
+    forward(1, INNER, 0, ROWS)
+    for i in range(2):
+        for copy in far_copies(i):
+            copy.start()
+            halos.append(copy)
+    lax.fori_loop(EARLY, CELL_ROWS // TILE, spread, 0)
+    for c, (first, size) in enumerate(CHUNKS):
+        for copy in rim_copies(u.at[2], 1, c):
+            copy.wait_recv()
+        forward(1, OUTER, first, size)
+        send_rims(u.at[3], 2, c)
+
+    forward(2, INNER, 0, ROWS)
+    for copy in lean:
+        copy.wait_recv()
+    for i in range(2):
+        for copy in far_copies(i):
+            copy.wait_recv()
+    for c, (first, size) in enumerate(CHUNKS):
+        for copy in rim_copies(u.at[3], 2, c):
+            copy.wait_recv()
+        forward(2, OUTER, first, size)
+        edge(*LAGGED[c])
+        forward(3, OUTER, *LAGGED[c])
+        send_rims(weighted.at[0], NT, c)
+    forward(3, INNER, 0, ROWS)
 
     half = pl.ds(pl.multiple_of(h * 256, 8), 256)
     kept = pl.ds(pl.multiple_of(PAD + 8 * h, 8), 256)
@@ -402,7 +461,7 @@
         if j == NT - 2:
             core_start(0)
             core_finish(0)
-        for c, (first, size) in enumerate(CHUNKS):
+        for c, (first, size) in enumerate(LAGGED):
             for copy in rim_copies(weighted.at[j], NT + j, c):
                 copy.wait_recv()
             backward(j, OUTER, first, size)
@@ -440,7 +499,7 @@
         for k in range(1, 4):
             ring_copy(part, k).wait_send()
 
-    for copy in exchange + passed + opening + rims + halos:
+    for copy in exchange + passed + opening + lean + rims + halos:
         copy.wait_send()
     store.wait()
     give.wait()
@@ -498,6 +557,9 @@
             pltpu.VMEM((3, PLANES, ROWS, 128), f32),
             pltpu.VMEM((3, PLANES, ROWS + 2 * PAD, 128), f32),
             pltpu.VMEM((7, 2, ROWS, 128), f32),
+            pltpu.VMEM((2, ROWS + 2 * PAD, 128), f32),
+            pltpu.VMEM((2, ROWS, 128), f32),
+            pltpu.VMEM((2, ROWS, 128), f32),
             pltpu.VMEM((2, 2, ROWS, 128), f32),
             pltpu.VMEM((1, 2048), jnp.int32),
             pltpu.VMEM((1, NT, 2048), f32),
@@ -517,6 +579,10 @@
             dma((2, 8)),
             dma((3,)),
             dma((3,)),
+            dma((2,)),
+            dma((2,)),
+            dma((2, 2)),
+            dma((2, 2)),
             dma((2,)),
             dma((2,)),
             dma((7, chunks, 2)),

time: 71.2 us -> 70.5 us (level)
  no operation moved by 1% of the time
where the time goes in v5:
time: 70.5 us; the launch traced here: 70.3 us
  Pallas kernels  69 us (98%)
  between operations  1.29 us (2%)
    pallas_call x1, Pallas kernels, shards(): pl.pallas_call(kernel, out_shape=(jax.ShapeDtypeStruct((2, 16, 128), f32)...  67.2 us
    pallas_call x1, Pallas kernels, shards(): pl.pallas_call(hand_over, out_shape=tuple((jax.ShapeDtypeStruct(r.shape,...  1.84 us

profile of v5, /device:TPU:1, one launch (start us, length us, event | category | flops | bytes accessed | tf_op | source)
XLA Modules:
  0.0 70.3 jit_solution(5896951603231750002)
XLA Ops:
  1.3 67.2 %window.1 = (f32[2,16,128]{2,1,0:T(8,128)}, f32[1,2,512,128]{3,2,1,0:T(8,128)}) custom-call(f32[2,512,128]{2,1,0:T(8,128)} %kappa_ref.1, f32[1,2,512,128]{3,2,1,0:T(8,128)} %now_ref.1, f32[1,2,512,128]{3,2,1,0:T(8,128)} %before_ref.1, f32[1,4]{1,0:T(1,128)} %wavelet_ref.1, s32[1]{0:T(128)S(6)} %copy.9.source_ref, s32[1,2048]{1,0:T(1,128)} %receiver_ref.1, ...), custom_call_target="tpu_custom_call" | custom-call | tf_op jit(solution)/shard_map/window/pallas_call | solution.py:544
  68.5 1.8 %hand_over.1 = (f32[2,16,128]{2,1,0:T(8,128)}, f32[1,2,512,128]{3,2,1,0:T(8,128)}) custom-call(f32[2,16,128]{2,1,0:T(8,128)} %get-tuple-element.4.gradient_ref, f32[1,2,512,128]{3,2,1,0:T(8,128)} %get-tuple-element.5.next_ref), custom_call_target="tpu_custom_call" | custom-call | tf_op jit(solution)/shard_map/hand_over/pallas_call | solution.py:603

commit v6 on v5

--- a/solution.py
+++ b/solution.py
@@ -177,20 +177,17 @@
     for copy in rims:
         copy.start()
 
-    passed = []
-
     def pass_on(i):
         part = model.at[(3 - 3 * h, 2 - h)[i], eighth]
         for k in range(1, 8):
-            copy = copy_to(stack_device(k)[1], part, part, share_send.at[i, k], share_recv.at[i, z])
+            copy = copy_to(stack_device(k)[1], part, part, share_send.at[i], share_recv.at[i, z])
             copy.start()
-            passed.append(copy)
 
     def take_over(i):
         for k in range(1, 8):
             at, device = stack_device(k)
             part = model.at[(3 - 3 * h, 2 - h)[i], share(at * 32, 32)]
-            copy_to(device, part, part, share_send.at[i, k], share_recv.at[i, at]).wait_recv()
+            copy_to(device, part, part, share_send.at[i], share_recv.at[i, at]).wait_recv()
 
     exchange[0].wait_recv()
     pass_on(0)
@@ -327,8 +324,8 @@
         at, to = pl.ds(PAD + first, size), pl.ds(first, size)
         into = (near.at[0, at], near.at[1, at]) if n == 2 else (halo.at[n, 0, to], halo.at[n, 1, to])
         return (
-            copy_to(above, field.at[PLANES - 1, at], into[0], halo_send.at[n, c, 0], halo_recv.at[n, c, 0]),
-            copy_to(below, field.at[0, at], into[1], halo_send.at[n, c, 1], halo_recv.at[n, c, 1]),
+            copy_to(above, field.at[PLANES - 1, at], into[0], halo_send.at[n], halo_recv.at[n, c, 0]),
+            copy_to(below, field.at[0, at], into[1], halo_send.at[n], halo_recv.at[n, c, 1]),
         )
 
     def far_copies(i):
@@ -344,7 +341,6 @@
     def send_rims(field, n, c):
         for copy in rim_copies(field, n, c):
             copy.start()
-            halos.append(copy)
 
     for load in loads[2:]:
         load.wait()
@@ -499,8 +495,13 @@
         for k in range(1, 4):
             ring_copy(part, k).wait_send()
 
-    for copy in exchange + passed + opening + lean + rims + halos:
+    for copy in exchange + opening + lean + rims + halos:
         copy.wait_send()
+    for n in (1, 2, 4, 5, 6):
+        copy_to(twin, halo.at[n], halo.at[n], halo_send.at[n], halo_recv.at[n, 0, 0]).wait_send()
+    for i in range(2):
+        rows = model.at[0, 0:224]
+        copy_to(twin, rows, rows, share_send.at[i], share_recv.at[i, 0]).wait_send()
     store.wait()
     give.wait()
     sent(0)
@@ -575,7 +576,7 @@
             dma((6,)),
             dma((8,)),
             dma((8,)),
-            dma((2, 8)),
+            dma((2,)),
             dma((2, 8)),
             dma((3,)),
             dma((3,)),
@@ -585,7 +586,7 @@
             dma((2, 2)),
             dma((2,)),
             dma((2,)),
-            dma((7, chunks, 2)),
+            dma((7,)),
             dma((7, chunks, 2)),
             dma((3,)),
             dma((2, 8)),

time: 70.5 us -> 69.7 us (0.989)
  Pallas kernels: 69 us -> 68.2 us
    pallas_call x1, Pallas kernels: 67.2 us -> 66.4 us  [shards(): pl.pallas_call(kernel, out_shape=(jax.ShapeDtypeStruct((2, 16, 128), f32)...]
where the time goes in v6:
time: 69.7 us; the launch traced here: 69.5 us
  Pallas kernels  68.2 us (98%)
  between operations  1.29 us (2%)
    pallas_call x1, Pallas kernels, shards(): pl.pallas_call(kernel, out_shape=(jax.ShapeDtypeStruct((2, 16, 128), f32)...  66.4 us
    pallas_call x1, Pallas kernels, shards(): pl.pallas_call(hand_over, out_shape=tuple((jax.ShapeDtypeStruct(r.shape,...  1.84 us

profile of v6, /device:TPU:1, one launch (start us, length us, event | category | flops | bytes accessed | tf_op | source)
XLA Modules:
  0.0 69.5 jit_solution(7630376400054694602)
XLA Ops:
  1.3 66.4 %window.1 = (f32[2,16,128]{2,1,0:T(8,128)}, f32[1,2,512,128]{3,2,1,0:T(8,128)}) custom-call(f32[2,512,128]{2,1,0:T(8,128)} %kappa_ref.1, f32[1,2,512,128]{3,2,1,0:T(8,128)} %now_ref.1, f32[1,2,512,128]{3,2,1,0:T(8,128)} %before_ref.1, f32[1,4]{1,0:T(1,128)} %wavelet_ref.1, s32[1]{0:T(128)S(6)} %copy.9.source_ref, s32[1,2048]{1,0:T(1,128)} %receiver_ref.1, ...), custom_call_target="tpu_custom_call" | custom-call | tf_op jit(solution)/shard_map/window/pallas_call | solution.py:545
  67.6 1.8 %hand_over.1 = (f32[2,16,128]{2,1,0:T(8,128)}, f32[1,2,512,128]{3,2,1,0:T(8,128)}) custom-call(f32[2,16,128]{2,1,0:T(8,128)} %get-tuple-element.4.gradient_ref, f32[1,2,512,128]{3,2,1,0:T(8,128)} %get-tuple-element.5.next_ref), custom_call_target="tpu_custom_call" | custom-call | tf_op jit(solution)/shard_map/hand_over/pallas_call | solution.py:604
